TPU v7x, 32 devices: a whole 2x2x4 slice. The times are simulated.
32 devices in a mesh: seq: 4 (over z), shard: 8 (over y, x, core).
Axes of the slice: x: 2, y: 2, z: 4, core: 2. Of those that a mesh axis runs over, the one named last changes fastest.
Arguments:
- hidden_in: bfloat16 [8192, 512], P(('shard', 'seq')), may hold values from -6 to 6
- encoder: bfloat16 [2048, 512], P(('shard', 'seq')), may hold values from -6 to 6
- segment_ids: int32 [8192], replicated, may hold values from 0 to 1, never falling along the last dimension, each value on 1 to 5120 neighbouring positions
- timestep: int32 [2], replicated, may hold values from 0 to 49
- out_grad: bfloat16 [8192, 512], P(('shard', 'seq')), may hold values from -6 to 6
- time_table: bfloat16 [50, 512], P(None, 'shard'), may hold values from -6 to 6
- norm_gain: bfloat16 [3, 512], P(None, 'shard'), may hold values from 0.5 to 1.5
- norm_bias: bfloat16 [3, 512], P(None, 'shard'), may hold values from -1.5 to 1.5
- self_proj: bfloat16 [512, 1536], P('shard'), may hold values from -0.25 to 0.25
- self_out: bfloat16 [512, 512], P('shard'), may hold values from -1 to 1
- cross_query: bfloat16 [512, 512], P('shard'), may hold values from -0.25 to 0.25
- cross_memory: bfloat16 [512, 1024], P('shard'), may hold values from -0.25 to 0.25
- cross_out: bfloat16 [512, 512], P('shard'), may hold values from -1 to 1
- up_weight: bfloat16 [512, 2048], P('shard'), may hold values from -0.25 to 0.25
- up_bias: bfloat16 [2048], P('shard'), may hold values from -2.5 to 2.5
- down_weight: bfloat16 [2048, 512], P('shard'), may hold values from -0.125 to 0.125
- down_bias: bfloat16 [512], P('shard'), may hold values from -1.5 to 1.5
Outputs:
- layer_out: bfloat16 [8192, 512], P(('shard', 'seq'))
- hidden_grad: float32 [8192, 512], P(('shard', 'seq'))
- encoder_grad: float32 [2048, 512], P(('shard', 'seq'))
- time_grad: float32 [50, 512], P(None, 'shard')
- gain_grad: float32 [3, 512], P(None, 'shard')
- bias_grad: float32 [3, 512], P(None, 'shard')
- proj_grad: float32 [512, 1536], P('shard')
- self_out_grad: float32 [512, 512], P('shard')
- query_grad: float32 [512, 512], P('shard')
- memory_grad: float32 [512, 1024], P('shard')
- cross_out_grad: float32 [512, 512], P('shard')
- up_weight_grad: float32 [512, 2048], P('shard')
- up_bias_grad: float32 [2048], P('shard')
- down_weight_grad: float32 [2048, 512], P('shard')
- down_bias_grad: float32 [512], P('shard')
Inputs may be any that keep to these rules, and one draw needn't show every extreme that they name: `segment_ids`: never falling; 2 sequences of 1 to 5120 tokens each.
All inputs are finite; a program needn't handle non-finite values.
Results may differ from a plain program's by a relative error of at most 0.023.
Values may be sent and summed in bfloat16 or wider, within the bound.
A program may use at most 256 MiB of HBM per device.

v0:
```python
import functools

import jax
import jax.numpy as jnp
from jax import lax
from jax.experimental import pallas as pl
from jax.experimental.pallas import tpu as pltpu
from jax.sharding import PartitionSpec as P

H = 8
HD = 64
DOCS = 2
ENC = 1024
EPS = 1e-05
MASKED = -1e30
SCALE = HD**-0.5
MESH = pl.DeviceIdType.MESH
BF = jnp.bfloat16
F32 = jnp.float32
DMA = pltpu.SemaphoreType.DMA


def room(small=True):
    return (ROOM << 20) if small and lax.axis_size("shard") == 8 else (63 << 20)


ROOM = 30
ORDER = (0, 1, 2, 4, 3, 6, 5, 7)


def mm(a, b, ca=1, cb=0):
    return lax.dot_general(a, b, (((ca,), (cb,)), ((), ())), preferred_element_type=F32)


def flip(j, bits):
    low, mid, high = j % 2, (j // 2) % 2, (j // 4) % 2
    out = j
    if bits & 1:
        out = out + 1 - 2 * low
    if bits & 2:
        out = out + 2 - 4 * mid
    if bits & 4:
        out = out + 4 - 8 * high
    return out


def rcopy(src, dst, send_sem, recv_sem, device_id):
    return pltpu.make_async_remote_copy(
        src_ref=src,
        dst_ref=dst,
        send_sem=send_sem,
        recv_sem=recv_sem,
        device_id=device_id,
        device_id_type=MESH,
    )


def place():
    shard, seq = lax.axis_index("shard"), lax.axis_index("seq")
    return shard, seq, shard % 8, shard // 8


def greet(peers):
    barrier = pltpu.get_barrier_semaphore()
    count = 0
    for condition, device in peers:
        if condition is None:
            pl.semaphore_signal(barrier, inc=1, device_id=device, device_id_type=MESH)
            count = count + 1
        else:

            @pl.when(condition)
            def _(device=device):
                pl.semaphore_signal(barrier, inc=1, device_id=device, device_id_type=MESH)

            count = count + jnp.where(condition, 1, 0)
    pl.semaphore_wait(barrier, count)


def norm_stats(value):
    center = jnp.mean(value, axis=1, keepdims=True)
    offset = value - center
    spread = jnp.mean(offset * offset, axis=1, keepdims=True)
    scale = lax.rsqrt(spread + EPS)
    return offset * scale, scale


def norm_back(d_out, hat, scale, gain):
    d_hat = d_out * gain
    first = jnp.mean(d_hat, axis=1, keepdims=True)
    second = jnp.mean(d_hat * hat, axis=1, keepdims=True)
    d_in = scale * (d_hat - first - hat * second)
    return d_in, jnp.sum(d_out * hat, axis=0, keepdims=True), jnp.sum(d_out, axis=0, keepdims=True)


def embed(hid_ref, bound, vecs_ref, block):
    rows = hid_ref.shape[0]
    pos = block * rows + lax.broadcasted_iota(jnp.int32, (rows, 1), 0)
    picked = jnp.where(pos < bound, vecs_ref[0:1, :], vecs_ref[1:2, :])
    return hid_ref[...].astype(F32) + picked


class Whole:
    def __init__(self, pairs, S, sems):
        self.pairs, self.S = pairs, S
        self.local, self.send, self.recv, self.half, self.pass_on = sems
        self.s = lax.axis_index("shard")
        self.core, self.chip = self.s % 2, self.s // 2
        self.sib = flip(self.s, 1)
        self.near = S == 8
        self.flow = []

    @staticmethod
    def scratch(count, S):
        return [DMA((count,)), DMA((count, max(8, S // 2))), DMA((count, S)), DMA((count, 2)), DMA((count, S // 2))]

    def copy(self, a, source, n, to, half=None):
        shard, whole = self.pairs[a]
        target = whole.at[source]
        if half is not None:
            rows = shard.shape[0] // 2
            target = whole.at[source, pl.ds(half * rows, rows)]
            recv = self.half.at[a, half]
        else:
            recv = self.recv.at[a, source]
        origin = shard if n < 0 else target
        send = self.send.at[a, -n - 1 if n < 0 else n]
        return rcopy(origin, target, send, recv, {"shard": to})

    def go(self, *args):
        c = self.copy(*args)
        c.start()
        self.flow.append(c)

    def arrived(self, a, source, half=None):
        self.copy(a, source, 7, self.sib, half).wait_recv()

    def same_core(self, d):
        return ((self.chip + d) % (self.S // 2)) * 2 + self.core

    def start(self, a):
        shard, whole = self.pairs[a]
        pltpu.make_async_copy(shard, whole.at[self.s], self.local.at[a]).start()
        s = self.s
        if self.near:
            self.go(a, s, -1, flip(s, 2))
            self.go(a, s, -2, flip(s, 4))
            self.go(a, s, -3, self.sib)
            return
        for d in range(1, self.S // 2):
            c = rcopy(shard, whole.at[s], self.send.at[a, d], self.recv.at[a, s], {"shard": self.same_core(d)})
            c.start()
            self.flow.append(c)
        c = rcopy(shard, whole.at[s], self.send.at[a, 0], self.recv.at[a, s], {"shard": self.sib})
        c.start()
        self.flow.append(c)

    def relay(self, a):
        if not self.near:
            return
        x, y = flip(self.s, 2), flip(self.s, 4)
        self.arrived(a, x)
        self.go(a, x, 3, y, 0)
        self.go(a, x, 5, self.sib)
        self.arrived(a, y)
        self.go(a, y, 4, x, 1)
        self.go(a, y, 6, self.sib)

    def finish(self, a):
        if self.near:
            far = flip(self.s, 6)
            self.arrived(a, far, 0)
            self.arrived(a, far, 1)
            self.go(a, far, 7, self.sib)
            return
        _, whole = self.pairs[a]
        for d in range(1, self.S // 2):
            q = self.same_core(self.S // 2 - d)
            self.arrived(a, q)
            c = rcopy(whole.at[q], whole.at[q], self.pass_on.at[a, d], self.recv.at[a, q], {"shard": self.sib})
            c.start()
            self.flow.append(c)

    def wait(self, a):
        shard, whole = self.pairs[a]
        self.arrived(a, self.sib)
        for d in range(1, self.S // 2):
            self.arrived(a, flip(self.same_core(d), 1))
        pltpu.make_async_copy(shard, whole.at[self.s], self.local.at[a]).wait()

    def drain(self):
        for c in self.flow:
            c.wait_send()


def gather_kernel(
    S, Z, G,
    timestep, seg_h, hid_h, table_h, gain_h, shift_h, upb_h, dnb_h, wproj_h, wmem_h, enc_h,
    wout, wcq, wco, wup, wdn,
    info, x_all, kv, qt, mkv, enc_all, vecs, upb_row, gout, gcq, gco, gup, gdn,
    seg, hid, table, gain, shift, upb, dnb, wproj, wmem, enc, in_sem,
    rows_f, small, small_all, wsend, msend, w_all, m_all, sm_s, sm_r, w_s, w_r, mw_s, mw_r,
    x_s, x_r, e_s, e_r, z_s, z_r, mb_s, mb_r, *whole_sems
):
    s, z, j, m = place()
    near = (seg, hid, table, gain, shift, upb, dnb, wproj, wmem, enc)
    far = (seg_h, hid_h, table_h, gain_h, shift_h, upb_h, dnb_h, wproj_h, wmem_h, enc_h)
    loads = [pltpu.make_async_copy(b, a, in_sem.at[n]) for n, (a, b) in enumerate(zip(near, far))]
    for c in loads:
        c.start()
    for c in loads:
        c.wait()
    R, F = wproj.shape[0], upb.shape[0]
    T, E = hid.shape[0], enc.shape[0]
    sib = flip(s, 1)

    step = lax.broadcasted_iota(jnp.int32, table.shape, 0)
    rows_f[...] = jnp.zeros((16, 256), F32)
    for d in range(DOCS):
        picked = jnp.where(step == timestep[d], table[...].astype(F32), 0.0)
        rows_f[d : d + 1, :R] = jnp.sum(picked, axis=0, keepdims=True)
    rows_f[2:5, :R] = gain[...].astype(F32)
    rows_f[5:8, :R] = shift[...].astype(F32)
    rows_f[8:9, :F] = upb[...].astype(F32).reshape(1, F)
    rows_f[9:10, :R] = dnb[...].astype(F32).reshape(1, R)
    small[...] = rows_f[...].astype(BF)
    small_all[s] = small[...]
    bound = jnp.sum(jnp.where(seg[...] == 0, 1.0, 0.0)).astype(jnp.int32)
    info[0] = bound
    info[1] = m
    info[2] = z
    info[3] = s

    greet(
        [(None, {"shard": (s + d) % S}) for d in range(1, S)]
        + [(z > 0, {"seq": z - 1}), (z < Z - 1, {"seq": z + 1})]
    )
    small_copies = []
    for d in range(1, S):
        c = rcopy(small, small_all.at[s], sm_s.at[d], sm_r.at[s], {"shard": (s + d) % S})
        c.start()
        small_copies.append(c)
    for h in range(H):
        k = wproj[:, 512 + HD * h : 512 + HD * (h + 1)]
        v = wproj[:, 1024 + HD * h : 1024 + HD * (h + 1)]
        q = wproj[:, HD * h : HD * (h + 1)]
        wsend[h] = jnp.concatenate([k, v, q, jnp.zeros_like(q)], axis=1)
        msend[h] = jnp.concatenate(
            [wmem[:, HD * h : HD * (h + 1)], wmem[:, 512 + HD * h : 512 + HD * (h + 1)]], axis=1
        )
    w_all[s] = wsend[j]
    m_all[s] = msend[j]
    w_copies = []
    for d in range(1, S):
        p = (s + d) % S
        c = rcopy(wsend.at[p % 8], w_all.at[s], w_s.at[d], w_r.at[s], {"shard": p})
        c.start()
        w_copies.append(c)
        c = rcopy(msend.at[p % 8], m_all.at[s], mw_s.at[d], mw_r.at[s], {"shard": p})
        c.start()
        w_copies.append(c)
    for d in range(1, S):
        p = (s + d) % S
        rcopy(small, small_all.at[p], sm_s.at[d], sm_r.at[p], {"shard": p}).wait_recv()
    rows = jnp.zeros((16, 512), F32)
    lane = lax.broadcasted_iota(jnp.int32, (256, 512), 0)
    col = lax.broadcasted_iota(jnp.int32, (256, 512), 1)
    for p in range(S):
        pick = ((col - p * R) == lane) & (lane < R)
        rows = rows + mm(small_all[p], jnp.where(pick, 1.0, 0.0).astype(BF))
        upb_row[0:1, p * F : (p + 1) * F] = small_all[p].astype(F32)[8:9, :F]
    vecs[...] = rows

    hat, _ = norm_stats(embed(hid, bound, vecs, s * Z + z))
    x_all[j] = (hat * vecs[2:3, :] + vecs[5:6, :]).astype(BF)
    enc_all[j] = enc[...]
    copies = []

    def send_block(ref, bits_source, bits_target, send, recv):
        source = flip(j, bits_source)
        c = rcopy(ref.at[source], ref.at[source], send, recv.at[source], {"shard": flip(s, bits_target)})
        c.start()
        copies.append(c)

    def wait_block(ref, bits, recv):
        source = flip(j, bits)
        rcopy(ref.at[source], ref.at[source], x_s.at[0], recv.at[source], {"shard": sib}).wait_recv()

    for n, bits in enumerate((1, 2, 4, 6)):
        send_block(x_all, 0, bits, x_s.at[n], x_r)
    for n, bits in enumerate((1, 2, 4, 6)):
        send_block(enc_all, 0, bits, e_s.at[n], e_r)
    whole = Whole(
        ((wout, gout), (wcq, gcq), (wco, gco), (wup, gup), (wdn, gdn)), S, whole_sems
    )
    for d in range(1, S):
        p = (s + d) % S
        rcopy(wsend.at[0], w_all.at[p], w_s.at[d], w_r.at[p], {"shard": p}).wait_recv()
        rcopy(msend.at[0], m_all.at[p], mw_s.at[d], mw_r.at[p], {"shard": p}).wait_recv()
    w_head = w_all[...].reshape(S * R, 256)
    m_head = m_all[...].reshape(S * R, 128)

    def z_copy(ref, block, plane, step, hop, slot):
        view = ref.at[:, block, plane] if block is not None else ref.at[:, :, plane]
        way = (step + 1) // 2
        return rcopy(view, view, z_s.at[way, hop, slot], z_r.at[way, hop, slot], {"seq": z + step})

    def z_passes(step, hop):
        origin = z - step * hop
        return (z + step >= 0) & (z + step < Z) & (origin >= 0) & (origin < Z)

    def z_send(ref, block, hop, slot):
        for step in (-1, 1):

            @pl.when(z_passes(step, hop))
            def _(step=step):
                z_copy(ref, block, z - step * hop, step, hop, slot).start()

    def z_recv(ref, block, hop, slot):
        for step in (-1, 1):
            origin = z - step * hop

            @pl.when((origin >= 0) & (origin < Z))
            def _(step=step, origin=origin):
                z_copy(ref, block, origin, step, hop - 1, slot).wait_recv()

    def z_drain(ref, block, hop, slot):
        for step in (-1, 1):

            @pl.when(z_passes(step, hop))
            def _(step=step):
                z_copy(ref, block, z - step * hop, step, hop, slot).wait_send()

    def member_copy(ref, block, d, slot, mine):
        other = (m + d) % G
        at = m if mine else other
        view = ref.at[at, block, z] if block is not None else ref.at[at, :, z]
        return rcopy(view, view, mb_s.at[d, slot], mb_r.at[at, slot], {"shard": other * 8 + j})

    def spread(ref, block, slot):
        for d in range(1, G):
            member_copy(ref, block, d, slot, True).start()
        for d in range(1, G):
            member_copy(ref, block, d, slot, False).wait_recv()
        z_send(ref, block, 0, slot)

    def block_step(n):
        bits = ORDER[n]
        block = flip(j, bits)
        if bits:
            wait_block(x_all, bits, x_r)
            if bits in (2, 4, 6):
                send_block(x_all, bits, 1, x_s.at[3 + bits // 2], x_r)
        kvq = mm(x_all[block], w_head)
        kv[m, block, z] = kvq[:, :128].astype(BF)
        spread(kv, block, n)
        qt[block] = (SCALE * kvq[:, 128:256].T[:HD]).astype(BF)

    def encoder_step():
        for bits in (2, 4, 6):
            wait_block(enc_all, bits, e_r)
            send_block(enc_all, bits, 1, e_s.at[3 + bits // 2], e_r)
        for bits in (1, 3, 5, 7):
            wait_block(enc_all, bits, e_r)
        for b in range(8):
            mkv[b] = mm(enc_all[b], m_head).astype(BF)

    lag = 2
    last_step = max(8, 7 + lag * (Z - 1))
    for n in range(last_step + 1):
        if n < 8:
            block_step(n)
        if n == 8:
            encoder_step()
        if n == 5:
            for a in range(5):
                whole.start(a)
        for hop in range(1, Z):
            slot = n - lag * hop
            if 0 <= slot < 8:
                z_recv(kv, flip(j, ORDER[slot]), hop, slot)
                z_send(kv, flip(j, ORDER[slot]), hop, slot)
        if n == 8:
            for a in range(3):
                whole.relay(a)
        if n == min(10, last_step):
            whole.relay(3)
        if n == min(11, last_step):
            whole.relay(4)
        if n == min(12, last_step):
            for a in range(3):
                whole.finish(a)
    for a in range(3, 5):
        whole.finish(a)
    for a in range(5):
        whole.wait(a)
    whole.drain()
    for c in small_copies + w_copies + copies:
        c.wait_send()
    for n, bits in enumerate(ORDER):
        for d in range(1, G):
            member_copy(kv, flip(j, bits), d, n, True).wait_send()
        for hop in range(Z - 1):
            z_drain(kv, flip(j, bits), hop, n)


def gather_call(S, Z, args):
    G = S // 8
    (timestep, seg, hid, table, gain, shift, upb, dnb, wproj, wmem, enc, *weights) = args
    T, R, E, F = hid.shape[0], wproj.shape[0], enc.shape[0], upb.shape[0]
    vmem = pl.BlockSpec(memory_space=pltpu.VMEM)
    smem = pl.BlockSpec(memory_space=pltpu.SMEM)
    hbm = pl.BlockSpec(memory_space=pl.ANY)
    sds = jax.ShapeDtypeStruct
    outs = [
        sds((4,), jnp.int32),
        sds((8, T, 512), BF),
        sds((G, 8, Z, T, 128), BF),
        sds((8, HD, T), BF),
        sds((8, E, 128), BF),
        sds((8, E, 512), BF),
        sds((16, 512), F32),
        sds((1, S * F), F32),
    ] + [sds((S,) + w.shape, BF) for w in weights]
    return pl.pallas_call(
        functools.partial(gather_kernel, S, Z, G),
        out_shape=outs,
        in_specs=[smem] + [pl.BlockSpec(memory_space=pltpu.HBM)] * (len(args) - 1),
        out_specs=[smem] + [vmem] * 7 + [hbm] * 5,
        scratch_shapes=[pltpu.VMEM(a.shape, a.dtype) for a in args[1:11]]
        + [
            DMA((10,)),
            pltpu.VMEM((16, 256), F32),
            pltpu.VMEM((16, 256), BF),
            pltpu.VMEM((S, 16, 256), BF),
            pltpu.VMEM((8, R, 256), BF),
            pltpu.VMEM((8, R, 128), BF),
            pltpu.VMEM((S, R, 256), BF),
            pltpu.VMEM((S, R, 128), BF),
            DMA((S,)), DMA((S,)), DMA((S,)), DMA((S,)), DMA((S,)), DMA((S,)),
            DMA((8,)), DMA((8,)), DMA((8,)), DMA((8,)),
            DMA((2, Z, 9)), DMA((2, Z, 9)),
            DMA((G, 9)), DMA((G, 9)),
        ] + Whole.scratch(5, S),
        compiler_params=pltpu.CompilerParams(
            collective_id=0, has_side_effects=True, vmem_limit_bytes=room()
        ),
        name="gather_qkv",
    )(args[0], *[pltpu.with_memory_space_constraint(a, pltpu.HBM) for a in args[1:]])


GROUP = 4


class Reach:
    def __init__(self, causal, bound, block, rows):
        self.causal, self.bound, self.rows = causal, bound, rows
        self.query_first = block * rows
        last = self.query_first + rows - 1
        mixed = (self.query_first < bound) & (last >= bound)
        if causal:
            self.least = jnp.where(self.query_first < bound, 0, bound)
            begin, self.end = self.least // rows, block + 1
            self.mixed = mixed | (self.end < GROUP)
        else:
            per = ENC // rows
            self.least = 0
            begin = jnp.where(self.query_first < bound, 0, per)
            self.end = jnp.where(last < bound, per, 2 * per)
            self.mixed = mixed
        self.groups = (self.end - begin + GROUP - 1) // GROUP

    def mask(self, kind, start, limit, n, scores):
        if kind == "plain":
            return scores
        rows = self.rows
        key = (start + n) * rows + lax.broadcasted_iota(jnp.int32, (rows, 1), 0)
        query = self.query_first + lax.broadcasted_iota(jnp.int32, (1, scores.shape[1]), 1)
        if kind == "edge":
            allowed = (key >= self.least) & (key < limit)
            if n == GROUP - 1:
                allowed = allowed & (key <= query)
        elif self.causal:
            least = jnp.where(query < self.bound, 0, self.bound)
            allowed = (key < limit) & (key <= query) & (key >= least)
        else:
            allowed = jnp.where(query < self.bound, 0, 1) == key // ENC
        return jnp.where(allowed, scores, MASKED)

    def walk(self, group, state):
        def turn(kind, g, carry):
            if kind == "edge":
                g = jnp.where(g == 0, 0, self.groups - 1)
            stop = self.end - GROUP * (self.groups - 1 - g)
            return group(kind, jnp.maximum(stop - GROUP, 0), stop * self.rows, carry)

        mixed, groups = self.mixed, self.groups
        state = lax.fori_loop(
            0, jnp.where(mixed, groups, 0), functools.partial(turn, "full"), state
        )
        if not self.causal:
            return lax.fori_loop(
                0, jnp.where(mixed, 0, groups), functools.partial(turn, "plain"), state
            )
        state = lax.fori_loop(
            0,
            jnp.where(mixed, 0, jnp.minimum(groups, 2)),
            functools.partial(turn, "edge"),
            state,
        )
        return lax.fori_loop(
            1, jnp.where(mixed, 1, groups - 1), functools.partial(turn, "plain"), state
        )


def turned_keys(kv, kt, half, begin, end):
    rows = kv.shape[1]

    def turn(kb, carry):
        flat = kv[kb].astype(F32).T[HD * half : HD * (half + 1)].astype(BF)
        kt[:, pl.ds(pl.multiple_of(kb * rows, rows), rows)] = flat
        return carry

    lax.fori_loop(begin, end, turn, 0)


def key_span(causal, bound, low, Z, rows, count):
    if not causal:
        return 0, count
    return jnp.where(low * rows < bound, 0, bound) // rows, low + 7 * Z + 1


def attend_kernel(Z, causal, info, qt, kv, ot, of, lse, vt):
    bound, m, z = info[0], info[1], info[2]
    count, T = kv.shape[0], kv.shape[1]
    low = 8 * m * Z + z

    begin, end = key_span(causal, bound, low, Z, T, count)
    turned_keys(kv, vt, 1, jnp.maximum(begin - GROUP, 0), end)

    def one_block(i, carry):
        reach = Reach(causal, bound, low + i * Z, T)
        queries = jnp.concatenate([qt[i], jnp.zeros((HD, T), BF)], axis=0)

        def group(kind, start, limit, state):
            top, total, acc = state
            half = GROUP // 2
            raws = [
                mm(kv[pl.ds(start + half * h, half)].reshape(half * T, 128), queries) for h in range(2)
            ]
            for h, raw in enumerate(raws):
                scores = [
                    reach.mask(kind, start, limit, half * h + n, raw[n * T : (n + 1) * T])
                    for n in range(half)
                ]
                new_top = top
                for piece in scores:
                    new_top = jnp.maximum(new_top, jnp.max(piece, axis=0, keepdims=True))
                fade = jnp.exp(top - new_top)
                total = total * fade
                parts = []
                for piece in scores:
                    powers = jnp.exp(piece - new_top)
                    total = total + jnp.sum(powers, axis=0, keepdims=True)
                    parts.append(powers.astype(BF))
                values = vt[:, pl.ds(pl.multiple_of((start + half * h) * T, T), half * T)]
                acc = acc * fade + mm(values, jnp.concatenate(parts, axis=0))
                top = new_top
            return top, total, acc

        top, total, acc = reach.walk(
            group,
            (jnp.full((1, T), MASKED, F32), jnp.zeros((1, T), F32), jnp.zeros((HD, T), F32)),
        )
        result = acc / total
        ot[i] = result.astype(BF)
        of[i] = result
        lse[i] = top + jnp.log(total)
        return carry

    lax.fori_loop(0, 8, one_block, 0)


def attend(Z, causal, info, qt, kv):
    T = qt.shape[2]
    sds = jax.ShapeDtypeStruct
    vmem = pl.BlockSpec(memory_space=pltpu.VMEM)
    return pl.pallas_call(
        functools.partial(attend_kernel, Z, causal),
        out_shape=[sds((8, HD, T), BF), sds((8, HD, T), F32), sds((8, 1, T), F32)],
        in_specs=[pl.BlockSpec(memory_space=pltpu.SMEM), vmem, vmem],
        out_specs=[vmem] * 3,
        scratch_shapes=[pltpu.VMEM((HD, kv.shape[0] * T), BF)],
        compiler_params=pltpu.CompilerParams(vmem_limit_bytes=room()),
        name="attend_self" if causal else "attend_cross",
    )(info, qt, kv)


def attend_back_kernel(
    Z, causal, info, qt, kv, dt, of, lse, dq, dkv, kt, dkvf, qd, rows, raw, pair, stage, sem
):
    bound, m, z = info[0], info[1], info[2]
    count, T = kv.shape[0], kv.shape[1]
    low = 8 * m * Z + z
    zero = jnp.zeros((HD, T), BF)

    def clear(kb, carry):
        dkvf[kb] = jnp.zeros((T, 128), F32)
        return carry

    lax.fori_loop(0, count, clear, 0)

    begin, end = key_span(causal, bound, low, Z, T, count)
    turned_keys(kv, kt, 0, jnp.maximum(begin - GROUP, 0), end)

    def one_block(i, carry):
        reach = Reach(causal, bound, low + i * Z, T)
        qd[:HD, :T] = qt[i]
        qd[HD:, :T] = zero
        qd[:HD, T:] = zero
        qd[HD:, T:] = dt[i]
        both = jnp.concatenate([qt[i].astype(F32), dt[i].astype(F32)], axis=0).T
        lane = lax.broadcasted_iota(jnp.int32, both.shape, 1)
        rows[:T] = jnp.where(lane < HD, 0.0, both).astype(BF)
        rows[T:] = jnp.where(lane < HD, both, 0.0).astype(BF)
        delta = jnp.sum(dt[i].astype(F32) * of[i], axis=0, keepdims=True)
        level = lse[i]

        def group(kind, start, limit, acc):
            keys = kv[pl.ds(start, GROUP)].reshape(GROUP * T, 128)
            raw[...] = mm(keys, qd[...])
            for n in range(GROUP):
                at = slice(n * T, (n + 1) * T)
                probs = jnp.exp(reach.mask(kind, start, limit, n, raw[at, :T]) - level)
                pair[at, :T] = probs.astype(BF)
                pair[at, T:] = (probs * (raw[at, T:] - delta)).astype(BF)
            grads = mm(pair[...], rows[...])
            dkvf[pl.ds(start, GROUP)] += grads.reshape(GROUP, T, 128)
            flat = kt[:, pl.ds(pl.multiple_of(start * T, T), GROUP * T)]
            return acc + mm(flat, pair[:, T:])

        acc = reach.walk(group, jnp.zeros((HD, T), F32))
        dq[i] = (SCALE * acc).astype(BF)
        return carry

    lax.fori_loop(0, 8, one_block, 0)

    slots = stage.shape[0]

    def put(kb):
        return pltpu.make_async_copy(stage.at[kb % slots], dkv.at[kb], sem.at[kb % slots])

    def flush(kb, carry):
        @pl.when(kb >= slots)
        def _():
            put(kb).wait()

        stage[kb % slots] = dkvf[kb].astype(BF)
        put(kb).start()
        return carry

    def settle(kb, carry):
        put(kb).wait()
        return carry

    lax.fori_loop(0, count, flush, 0)
    lax.fori_loop(0, slots, settle, 0)


def attend_back(Z, causal, info, qt, kv, dt, of, lse):
    T = qt.shape[2]
    count = kv.shape[0]
    slots = count if count <= 32 else 2
    sds = jax.ShapeDtypeStruct
    vmem = pl.BlockSpec(memory_space=pltpu.VMEM)
    return pl.pallas_call(
        functools.partial(attend_back_kernel, Z, causal),
        out_shape=[sds((8, HD, T), BF), sds(kv.shape, BF)],
        in_specs=[pl.BlockSpec(memory_space=pltpu.SMEM)] + [vmem] * 5,
        out_specs=[vmem, pl.BlockSpec(memory_space=pl.ANY)],
        scratch_shapes=[
            pltpu.VMEM((HD, count * T), BF),
            pltpu.VMEM((count, T, 128), F32),
            pltpu.VMEM((128, 2 * T), BF),
            pltpu.VMEM((2 * T, 128), BF),
            pltpu.VMEM((GROUP * T, 2 * T), F32),
            pltpu.VMEM((GROUP * T, 2 * T), BF),
            pltpu.VMEM((slots, T, 128), BF),
            DMA((slots,)),
        ],
        compiler_params=pltpu.CompilerParams(vmem_limit_bytes=room()),
        name="attend_self_back" if causal else "attend_cross_back",
    )(info, qt, kv, dt, of, lse)


def greet_group(heads=False):
    s, z, j, m = place()
    peers = [(None, {"shard": m * 8 + (j + d) % 8}) for d in range(1, 8)]
    if heads:
        peers = peers + [(None, device) for _, _, _, device in kin()]
    greet(peers)


def kin():
    s, z, j, m = place()
    G, Z = lax.axis_size("shard") // 8, lax.axis_size("seq")
    out = []
    for dm in range(G):
        for dz in range(Z):
            if dm or dz:
                om, oz = (m + dm) % G, (z + dz) % Z
                out.append((dm * Z + dz, om, oz, {"shard": om * 8 + j, "seq": oz}))
    return out


def exchange_copies(src, dst, send, recv):
    s, z, j, m = place()
    out = []
    for d in (1, 2, 3, 4, 5, 6, 7):
        p = flip(j, d)
        out.append(rcopy(src.at[p], dst.at[j], send.at[d], recv.at[j], {"shard": m * 8 + p}))
    return out


def exchange_start(src, dst, send, recv):
    s, z, j, m = place()
    for c in exchange_copies(src, dst, send, recv):
        c.start()
    dst[j] = src[j]


def exchange_recv(src, dst, send, recv):
    s, z, j, m = place()
    for d in (1, 2, 3, 4, 5, 6, 7):
        p = flip(j, d)
        rcopy(src.at[p], dst.at[p], send.at[d], recv.at[p], {"shard": m * 8 + p}).wait_recv()


def exchange_sent(src, dst, send, recv):
    for c in exchange_copies(src, dst, send, recv):
        c.wait_send()


class ChipSums:
    def __init__(self, pairs, send, recv):
        self.pairs, self.send, self.recv = pairs, send, recv
        self.s = lax.axis_index("shard")
        self.core = self.s % 2
        self.chips = lax.axis_size("shard") // 2

    def piece(self, a, p):
        full, kept, _ = self.pairs[a]
        rows = kept.shape[1]
        return full.at[pl.ds(pl.multiple_of(p * rows, rows), rows), :]

    def copies(self):
        for a, (_, kept, buf) in enumerate(self.pairs):
            for q in range(self.chips):
                yield rcopy(
                    self.piece(a, 2 * q + 1 - self.core), buf.at[q], self.send.at[a, q], self.recv.at[a, q],
                    {"shard": flip(self.s, 1)},
                )

    def start(self):
        for c in self.copies():
            c.start()

    def finish(self):
        for c in self.copies():
            c.wait_recv()
        for a, (_, kept, buf) in enumerate(self.pairs):
            for q in range(self.chips):
                mine = self.piece(a, 2 * q + self.core)[...]
                kept[q] = (buf[q].astype(F32) + mine.astype(F32)).astype(BF)
        for c in self.copies():
            c.wait_send()


def remote_call(kernel, name, ident, ins, outs, scratch, smem=1, far=(), far_outs=()):
    vmem = pl.BlockSpec(memory_space=pltpu.VMEM)
    in_specs = [pl.BlockSpec(memory_space=pltpu.SMEM)] * smem + [vmem] * (len(ins) - smem)
    out_specs = [vmem] * len(outs)
    for n in far_outs:
        out_specs[n] = pl.BlockSpec(memory_space=pl.ANY)
    for n in far:
        in_specs[n] = pl.BlockSpec(memory_space=pl.ANY)
    return pl.pallas_call(
        kernel,
        out_shape=outs,
        in_specs=in_specs,
        out_specs=out_specs,
        scratch_shapes=scratch,
        compiler_params=pltpu.CompilerParams(
            collective_id=ident, has_side_effects=True, vmem_limit_bytes=room()
        ),
        name=name,
    )(*ins)


def middle_kernel(
    Z, bnd, ot, hid, vecs, wout, wcq, mem, at, after, n2, cqt, mkv, cq_send, s1, r1, s2, r2, s3, r3
):
    s, z, j, m = place()
    T = hid.shape[0]
    greet_group(True)
    exchange_start(ot, at, s1, r1)

    def memory_copies(mine):
        for n, om, oz, device in kin():
            c = m * Z + z if mine else om * Z + oz
            target = mkv.at[m, :, z] if mine else mkv.at[om, :, oz]
            yield rcopy(mem, target, s3.at[n], r3.at[c], device)

    for c in memory_copies(True):
        c.start()
    mkv[m, :, z] = mem[...]
    base = embed(hid, bnd[0], vecs, s * Z + z)
    exchange_recv(ot, at, s1, r1)
    attn = at[...].reshape(512, T).astype(F32).T.astype(BF)
    value = base + mm(attn, wout[...])
    after[...] = value
    hat, _ = norm_stats(value)
    normed = (hat * vecs[3:4, :] + vecs[6:7, :]).astype(BF)
    n2[...] = normed
    cq = mm(normed, wcq[...])
    cq_send[...] = (SCALE * cq.T).astype(BF).reshape(8, HD, T)
    exchange_start(cq_send, cqt, s2, r2)
    exchange_recv(cq_send, cqt, s2, r2)
    for c in memory_copies(False):
        c.wait_recv()
    exchange_sent(ot, at, s1, r1)
    exchange_sent(cq_send, cqt, s2, r2)
    for c in memory_copies(True):
        c.wait_send()


def middle(G, Z, bnd, ot, hid, vecs, wout, wcq, mem):
    T, E = hid.shape[0], mem.shape[1]
    sds = jax.ShapeDtypeStruct
    return remote_call(
        functools.partial(middle_kernel, Z),
        "middle",
        1,
        (bnd, ot, hid, vecs, wout, wcq, mem),
        [
            sds((8, HD, T), BF), sds((T, 512), F32), sds((T, 512), BF), sds((8, HD, T), BF),
            sds((G, 8, Z, E, 128), BF),
        ],
        [
            pltpu.VMEM((8, HD, T), BF), DMA((8,)), DMA((8,)), DMA((8,)), DMA((8,)),
            DMA((G * Z,)), DMA((G * Z,)),
        ],
    )


def erf(x):
    return lax.erf(x)


def feed_kernel(
    crt, after, vecs, upb, wco, wup, wdn, grad, wproj, wmem,
    layer_out, d_after, co_sum, up_sum, dn_sum, smalls, upb_grad, dct, gproj, gmem,
    ct, send, n3t, out_acc, dn_acc, co_grad, up_grad, dn_grad, co_buf, up_buf, dn_buf,
    s1, r1, s2, r2, s3, r3, *whole_sems
):
    T = after.shape[0]
    FF = wup.shape[1]
    S = lax.axis_size("shard")
    s = lax.axis_index("shard")
    greet([(None, {"shard": (s + d) % S}) for d in range(1, S)])
    exchange_start(crt, ct, s1, r1)
    whole = Whole(((wproj, gproj), (wmem, gmem)), S, whole_sems)
    for a in range(2):
        whole.start(a)
    g = grad[...]
    gf = g.astype(F32)
    gt = gf.T.astype(BF)
    exchange_recv(crt, ct, s1, r1)
    cross_t = ct[...].reshape(512, T)
    value = after[...] + mm(cross_t.astype(F32).T.astype(BF), wco[...])
    hat, scale = norm_stats(value)
    normed = hat * vecs[4:5, :] + vecs[7:8, :]
    n3 = normed.astype(BF)
    n3t[...] = n3.astype(F32).T.astype(BF)
    out_acc[...] = value + vecs[9:10, :]
    dn_acc[...] = jnp.zeros_like(dn_acc)
    width = 512
    for c in range(FF // width):
        lo, hi = c * width, (c + 1) * width
        pre = mm(n3, wup[:, lo:hi]) + upb[0:1, lo:hi]
        half = 0.5 * (1.0 + erf(pre * (0.5**0.5)))
        middle_c = (pre * half).astype(BF)
        out_acc[...] += mm(middle_c, wdn[lo:hi, :])
        slope = half + pre * (jnp.exp(-0.5 * pre * pre) * ((0.5 / jnp.pi) ** 0.5))
        d_pre = mm(g, wdn[lo:hi, :], 1, 1) * slope
        d_pre_b = d_pre.astype(BF)
        upb_grad[0:1, lo:hi] = jnp.sum(d_pre_b.astype(F32), axis=0, keepdims=True)
        dn_grad[lo:hi, :] = mm(middle_c.astype(F32).T.astype(BF), g).astype(BF)
        up_grad[:, lo:hi] = mm(n3t[...], d_pre_b).astype(BF)
        dn_acc[...] += mm(d_pre_b, wup[:, lo:hi], 1, 1)
    for a in range(2):
        whole.relay(a)
    layer_out[...] = out_acc[...].astype(BF)
    d_value, d_gain, d_shift = norm_back(dn_acc[...], hat, scale, vecs[4:5, :])
    total = gf + d_value
    d_after[...] = total
    smalls[0:1, :] = d_gain
    smalls[1:2, :] = d_shift
    smalls[2:3, :] = jnp.sum(gf, axis=0, keepdims=True)
    dc = total.astype(BF)
    d_cross = mm(wco[...], dc, 1, 1)
    send[...] = d_cross.astype(BF).reshape(8, HD, T)
    exchange_start(send, dct, s2, r2)
    co_grad[...] = mm(cross_t, dc).astype(BF)
    sums = ChipSums(
        ((co_grad, co_sum, co_buf), (up_grad, up_sum, up_buf), (dn_grad, dn_sum, dn_buf)), s3, r3
    )
    sums.start()
    for a in range(2):
        whole.finish(a)
    exchange_recv(send, dct, s2, r2)
    sums.finish()
    for a in range(2):
        whole.wait(a)
    whole.drain()
    exchange_sent(crt, ct, s1, r1)
    exchange_sent(send, dct, s2, r2)


def feed(crt, after, vecs, upb, wco, wup, wdn, grad, wproj, wmem):
    T, FF = after.shape[0], wup.shape[1]
    S = lax.axis_size("shard")
    chips, R, F = S // 2, 512 // S, FF // S
    sds = jax.ShapeDtypeStruct
    return remote_call(
        feed_kernel,
        "feed_forward",
        2,
        (crt, after, vecs, upb, wco, wup, wdn, grad, wproj, wmem),
        [
            sds((T, 512), BF),
            sds((T, 512), F32),
            sds((chips, R, 512), BF),
            sds((chips, R, FF), BF),
            sds((chips, F, 512), BF),
            sds((8, 512), F32),
            sds((1, FF), F32),
            sds((8, HD, T), BF),
            sds((S,) + wproj.shape, BF),
            sds((S,) + wmem.shape, BF),
        ],
        [
            pltpu.VMEM((8, HD, T), BF),
            pltpu.VMEM((8, HD, T), BF),
            pltpu.VMEM((512, T), BF),
            pltpu.VMEM((T, 512), F32),
            pltpu.VMEM((T, 512), F32),
            pltpu.VMEM((512, 512), BF),
            pltpu.VMEM((512, FF), BF),
            pltpu.VMEM((FF, 512), BF),
            pltpu.VMEM((chips, R, 512), BF),
            pltpu.VMEM((chips, R, FF), BF),
            pltpu.VMEM((chips, F, 512), BF),
            DMA((8,)), DMA((8,)), DMA((8,)), DMA((8,)), DMA((3, chips)), DMA((3, chips)),
        ] + Whole.scratch(2, S),
        smem=0,
        far_outs=(8, 9),
    )


def middle_back_kernel(
    dcqt, after, d_after2, n2, at, vecs, wcq, wout, dmkv,
    d_after, cq_sum, out_sum, smalls, dat, dmem,
    home, send, parts, cq_grad, out_grad, cq_buf, out_buf, s1, r1, s2, r2, s3, r3, s4, r4
):
    s, z, j, m = place()
    G, Z = dmkv.shape[0], dmkv.shape[2]
    T = after.shape[0]
    greet_group(True)
    exchange_start(dcqt, home, s1, r1)

    def memory_copies(mine):
        for n, om, oz, device in kin():
            c = m * Z + z if mine else om * Z + oz
            yield rcopy(dmkv.at[om, :, oz], parts.at[c], s3.at[n], r3.at[c], device)

    for c in memory_copies(True):
        c.start()
    parts[m * Z + z] = dmkv[m, :, z]
    hat, scale = norm_stats(after[...])
    n2t = n2[...].astype(F32).T.astype(BF)
    exchange_recv(dcqt, home, s1, r1)
    dcq = home[...].reshape(512, T).astype(F32).T.astype(BF)
    d_value, d_gain, d_shift = norm_back(mm(dcq, wcq[...], 1, 1), hat, scale, vecs[3:4, :])
    total = d_after2[...] + d_value
    d_after[...] = total
    smalls[0:1, :] = d_gain
    smalls[1:2, :] = d_shift
    da = total.astype(BF)
    send[...] = mm(wout[...], da, 1, 1).astype(BF).reshape(8, HD, T)
    exchange_start(send, dat, s2, r2)
    cq_grad[...] = mm(n2t, dcq).astype(BF)
    out_grad[...] = mm(at[...].reshape(512, T), da).astype(BF)
    sums = ChipSums(((cq_grad, cq_sum, cq_buf), (out_grad, out_sum, out_buf)), s4, r4)
    sums.start()
    for c in memory_copies(False):
        c.wait_recv()
    total_mem = parts[0].astype(F32)
    for n in range(1, G * Z):
        total_mem = total_mem + parts[n].astype(F32)
    dmem[...] = total_mem.astype(BF)
    sums.finish()
    exchange_recv(send, dat, s2, r2)
    exchange_sent(dcqt, home, s1, r1)
    exchange_sent(send, dat, s2, r2)
    for c in memory_copies(True):
        c.wait_send()


def middle_back(dcqt, after, d_after2, n2, at, vecs, wcq, wout, dmkv):
    T = after.shape[0]
    G, _, Z, E, _ = dmkv.shape
    chips, R = 4 * G, 512 // (8 * G)
    sds = jax.ShapeDtypeStruct
    return remote_call(
        middle_back_kernel,
        "middle_back",
        3,
        (dcqt, after, d_after2, n2, at, vecs, wcq, wout, dmkv),
        [
            sds((T, 512), F32),
            sds((chips, R, 512), BF),
            sds((chips, R, 512), BF),
            sds((8, 512), F32),
            sds((8, HD, T), BF),
            sds((8, E, 128), BF),
        ],
        [
            pltpu.VMEM((8, HD, T), BF),
            pltpu.VMEM((8, HD, T), BF),
            pltpu.VMEM((G * Z, 8, E, 128), BF),
            pltpu.VMEM((512, 512), BF),
            pltpu.VMEM((512, 512), BF),
            pltpu.VMEM((chips, R, 512), BF),
            pltpu.VMEM((chips, R, 512), BF),
            DMA((8,)), DMA((8,)), DMA((8,)), DMA((8,)), DMA((G * Z,)), DMA((G * Z,)),
            DMA((2, chips)), DMA((2, chips)),
        ],
        smem=0,
    )


NC = 16


def last_kernel(
    S, Z, G,
    info, hid, vecs, d_after, x_all, enc_all, dqt, dkv, finm, wproj, wmem,
    out_g, cq_g, co_g, up_g, dn_g, small2, small3, upb_g,
    hidden_grad, encoder_grad, zfin, smalls_o,
    got_out, got_cq, got_co, got_up, got_dn,
    rk, fin, mbuf, hkv, hq, hm, turned, enc_turned, dall, psend, pgot, msend, mgot,
    wz, zin, sm_all, sm_z, sm_plane, sm_mine,
    b_s, b_r, k_s, k_r, mb_s, mb_r, hq_s, hq_r, hk_s, hk_r, hm_s, hm_r,
    p_s, p_r, pm_s, pm_r, c_s, c_r, f_s, f_r, sm_s, sm_r, sz_s, sz_r,
):
    s, z, j, m = place()
    T, E = hid.shape[0], enc_all.shape[1]
    R = 512 // S
    F = dn_g.shape[1]
    bound = info[0]
    chips = S // 2
    core, chip = s % 2, s // 2
    sib = flip(s, 1)
    ends = (Z - 1, 0)
    greet(
        [(None, {"shard": (s + d) % S}) for d in range(1, S)]
        + [(None, {"seq": (z + d) % Z}) for d in range(1, Z)]
    )
    sums = (out_g, cq_g, co_g, up_g, dn_g)
    gots = (got_out, got_cq, got_co, got_up, got_dn)

    if G > 1:
        for d in range(1, G):
            o = (m + d) % G
            rcopy(dkv.at[o], mbuf.at[m], mb_s.at[d, 0], mb_r.at[m, 0], {"shard": o * 8 + j}).start()
        own_part = pltpu.make_async_copy(dkv.at[m], mbuf.at[m], mb_s.at[0, 0])
        own_part.start()
        own_part.wait()
        for d in range(1, G):
            o = (m + d) % G
            rcopy(dkv.at[o], mbuf.at[o], mb_s.at[d, 0], mb_r.at[o, 0], {"shard": o * 8 + j}).wait_recv()
        for b in range(8):
            acc = mbuf[m, b].astype(F32)
            for d in range(1, G):
                acc = acc + mbuf[(m + d) % G, b].astype(F32)
            mbuf[m, b] = acc.astype(BF)
        part = mbuf.at[m]
    else:
        part = dkv.at[0]

    def z_view(slot, t):
        return part.at[slot, t]

    def z_buffer(way, t, slot):
        return rk.at[way, t, slot]

    def z_copy(way, t, slot, source):
        step = 2 * way - 1
        return rcopy(
            source, z_buffer(way, t, slot), k_s.at[way, t, slot], k_r.at[way, t, slot], {"seq": z + step}
        )

    for far in range(Z - 1, 0, -1):
        for slot in range(8):
            for way in (0, 1):
                t = z + (2 * way - 1) * far

                @pl.when((z == ends[way]) & (t >= 0) & (t < Z))
                def _(way=way, t=t, slot=slot):
                    z_copy(way, t, slot, z_view(slot, t)).start()

    def own_copy(a, q):
        return rcopy(
            sums[a].at[q], gots[a].at[chip], b_s.at[a, q], b_r.at[a, chip], {"shard": 2 * q + core}
        )

    for a in range(5):
        for d in range(1, chips):
            own_copy(a, (chip + d) % chips).start()
    exchange_start(dqt, hq, hq_s, hq_r)
    exchange_start(finm, hm, hm_s, hm_r)

    def turn_block(b):
        turned[:, b * T : (b + 1) * T] = x_all[b].astype(F32).T.astype(BF)

    def turn_query(b):
        dq_b = dqt[b].astype(F32)
        dall[b * T : (b + 1) * T, 128:] = (
            jnp.concatenate([dq_b, jnp.zeros_like(dq_b)], axis=0).T.astype(BF)
        )

    def turn_encoder():
        enc_turned[...] = enc_all[...].reshape(8 * E, 512).astype(F32).T.astype(BF)

    def own_sum(a):
        for d in range(1, chips):
            q = (chip + d) % chips
            rcopy(sums[a].at[q], gots[a].at[q], b_s.at[a, q], b_r.at[a, q], {"shard": 2 * q + core}).wait_recv()
        total = sums[a][chip].astype(F32)
        for d in range(1, chips):
            total = total + gots[a][(chip + d) % chips].astype(F32)
        total = total.astype(BF)
        if a < 3:
            wz[a] = total
        elif a == 3:
            for c in range(4):
                wz[3 + c] = total[:, 512 * c : 512 * (c + 1)]
        else:
            for c in range(4):
                wz[7 + c] = total[c * R : (c + 1) * R]

    block = s * Z + z
    work = [functools.partial(turn_block, b) for b in range(8)]
    work += [functools.partial(turn_query, b) for b in range(8)] + [turn_encoder]

    for far in range(Z - 1, 0, -1):
        for slot in range(8):
            if work:
                work.pop(0)()
            for way in (0, 1):
                t = z + (2 * way - 1) * far

                @pl.when((z != ends[way]) & (t >= 0) & (t < Z))
                def _(way=way, t=t, slot=slot):
                    z_copy(way, t, slot, z_view(slot, t)).wait_recv()
                    buf = z_buffer(way, t, slot)
                    buf[...] = (
                        buf[...].astype(F32) + z_view(slot, t)[...].astype(F32)
                    ).astype(BF)
                    z_copy(way, t, slot, buf).start()

    def inward(k, step):
        way = (step + 1) // 2
        return rcopy(wz.at[k], zin.at[way, k], c_s.at[way, k], c_r.at[way, k], {"seq": z + step})

    def outward(k, step):
        return rcopy(zfin.at[k], zfin.at[k], f_s.at[(step + 1) // 2, k], f_r.at[k], {"seq": z + step})

    def root(k):
        return max(Z // 2 - 1 + k % 2, 0) if Z > 1 else 0

    def tips(k):
        r = root(k)
        for step in (-1, 1):
            tip = ends[(step + 1) // 2]
            if tip != r:

                @pl.when(z == tip)
                def _(step=step):
                    inward(k, step).start()

    def partial(k):
        r = root(k)
        for step, beyond in ((-1, z > r), (1, z < r)):
            tip = ends[(step + 1) // 2]
            way = (step + 1) // 2

            @pl.when(beyond & (z != tip))
            def _(step=step, way=way):
                inward(k, step).wait_recv()
                wz[k] = (wz[k].astype(F32) + zin[way, k].astype(F32)).astype(BF)
                inward(k, step).start()

    def total_of(k):
        r = root(k)

        @pl.when(z == r)
        def _():
            total = wz[k].astype(F32)
            if r < Z - 1:
                inward(k, -1).wait_recv()
                total = total + zin[0, k].astype(F32)
            if r > 0:
                inward(k, 1).wait_recv()
                total = total + zin[1, k].astype(F32)
            zfin[k] = total.astype(BF)
            if r < Z - 1:
                outward(k, 1).start()
            if r > 0:
                outward(k, -1).start()

    def send_out(k):
        r = root(k)
        for step, beyond in ((1, z > r), (-1, z < r)):
            tip = Z - 1 if step > 0 else 0

            @pl.when(beyond)
            def _(step=step, tip=tip):
                outward(k, step).wait_recv()

                @pl.when(z != tip)
                def _():
                    outward(k, step).start()

    for task in work:
        task()
    psend_q = mm(turned[...], dall[:, 128:])
    for a in range(5):
        own_sum(a)
        for k in ((0,), (1,), (2,), (3, 4, 5, 6), (7, 8, 9, 10))[a]:
            tips(k)
    hat, scale = norm_stats(embed(hid, bound, vecs, block))

    for slot in range(8):
        for way in (0, 1):

            @pl.when(z != ends[way])
            def _(way=way, slot=slot):
                z_copy(way, z, slot, z_view(slot, z)).wait_recv()

        low = jnp.where(z == ends[0], 0.0, z_buffer(0, z, slot)[...].astype(F32))
        high = jnp.where(z == ends[1], 0.0, z_buffer(1, z, slot)[...].astype(F32))
        total = (low + high + z_view(slot, z)[...].astype(F32)).astype(BF)
        fin[slot] = total
        dall[slot * T : (slot + 1) * T, :128] = total
    exchange_start(fin, hkv, hk_s, hk_r)
    for k in range(3):
        partial(k)

    psend_kv = mm(turned[...], dall[:, :128])
    psend[...] = jnp.concatenate([psend_kv, psend_q], axis=1).astype(BF).reshape(S, R, 256)
    msend[...] = mm(enc_turned[...], finm[...].reshape(8 * E, 128)).astype(BF).reshape(S, R, 128)
    pgot[s] = psend[s]
    mgot[s] = msend[s]
    for d in range(1, S):
        p = (s + d) % S
        rcopy(psend.at[p], pgot.at[s], p_s.at[d], p_r.at[s], {"shard": p}).start()
        rcopy(msend.at[p], mgot.at[s], pm_s.at[d], pm_r.at[s], {"shard": p}).start()

    for k in range(3):
        total_of(k)
    for k in range(3, 6):
        partial(k)

    exchange_recv(dqt, hq, hq_s, hq_r)
    exchange_recv(fin, hkv, hk_s, hk_r)
    exchange_recv(finm, hm, hm_s, hm_r)
    d_query = hq[...].reshape(512, T).astype(F32).T.astype(BF)
    d_keys = jnp.concatenate([hkv[h][:, :HD] for h in range(H)], axis=1)
    d_values = jnp.concatenate([hkv[h][:, HD:] for h in range(H)], axis=1)
    d_norm = (
        mm(d_query, wproj[:, :512], 1, 1)
        + mm(d_keys, wproj[:, 512:1024], 1, 1)
        + mm(d_values, wproj[:, 1024:], 1, 1)
    )
    d_value, d_gain, d_shift = norm_back(d_norm, hat, scale, vecs[2:3, :])
    total = d_after[...] + d_value
    hidden_grad[...] = total
    pos = block * T + lax.broadcasted_iota(jnp.int32, (T, 1), 0)
    sm_mine[...] = jnp.zeros((16, 512), F32)
    sm_mine[0:1, :] = d_gain
    sm_mine[1:2, :] = small2[0:1, :]
    sm_mine[2:3, :] = small3[0:1, :]
    sm_mine[3:4, :] = d_shift
    sm_mine[4:5, :] = small2[1:2, :]
    sm_mine[5:6, :] = small3[1:2, :]
    sm_mine[6:7, :] = jnp.sum(jnp.where(pos < bound, total, 0.0), axis=0, keepdims=True)
    sm_mine[7:8, :] = jnp.sum(jnp.where(pos < bound, 0.0, total), axis=0, keepdims=True)
    sm_mine[8:9, :] = small3[2:3, :]
    for c in range(upb_g.shape[1] // 512):
        sm_mine[9 + c : 10 + c, :] = upb_g[0:1, 512 * c : 512 * (c + 1)]
    for d in range(1, S):
        rcopy(sm_mine, sm_all.at[s], sm_s.at[d], sm_r.at[s], {"shard": (s + d) % S}).start()
    sm_all[s] = sm_mine[...]

    for k in range(6, 11):
        partial(k)
        total_of(k - 3)

    for d in range(1, S):
        p = (s + d) % S
        rcopy(psend.at[p], pgot.at[p], p_s.at[d], p_r.at[p], {"shard": p}).wait_recv()
        rcopy(msend.at[p], mgot.at[p], pm_s.at[d], pm_r.at[p], {"shard": p}).wait_recv()
    heads, mheads = [], []
    for h in range(H):
        acc, accm = pgot[h].astype(F32), mgot[h].astype(F32)
        for g in range(1, G):
            acc = acc + pgot[8 * g + h].astype(F32)
            accm = accm + mgot[8 * g + h].astype(F32)
        heads.append(acc)
        mheads.append(accm)
    wz[11] = jnp.concatenate([v[:, 128 : 128 + HD] for v in heads], axis=1).astype(BF)
    wz[12] = jnp.concatenate([v[:, :HD] for v in heads], axis=1).astype(BF)
    wz[13] = jnp.concatenate([v[:, HD:128] for v in heads], axis=1).astype(BF)
    wz[14] = jnp.concatenate([v[:, :HD] for v in mheads], axis=1).astype(BF)
    wz[15] = jnp.concatenate([v[:, HD:] for v in mheads], axis=1).astype(BF)
    for k in range(11, NC):
        tips(k)
    for k in range(8, 11):
        total_of(k)
    for k in range(6):
        send_out(k)
    e_keys = jnp.concatenate([hm[h][:, :HD] for h in range(H)], axis=1)
    e_values = jnp.concatenate([hm[h][:, HD:] for h in range(H)], axis=1)
    encoder_grad[...] = mm(e_keys, wmem[:, :512], 1, 1) + mm(e_values, wmem[:, 512:], 1, 1)

    for d in range(1, S):
        p = (s + d) % S
        rcopy(sm_mine, sm_all.at[p], sm_s.at[d], sm_r.at[p], {"shard": p}).wait_recv()
    acc = sm_all[0]
    for p in range(1, S):
        acc = acc + sm_all[p]
    sm_plane[...] = acc
    for d in range(1, Z):
        rcopy(sm_plane, sm_z.at[z], sz_s.at[d], sz_r.at[z], {"seq": (z + d) % Z}).start()
    sm_z[z] = acc
    for k in range(11, NC):
        partial(k)
        send_out(k - 5)
    for k in range(11, NC):
        total_of(k)
    for k in range(11, NC):
        send_out(k)
    for d in range(1, Z):
        o = (z + d) % Z
        rcopy(sm_plane, sm_z.at[o], sz_s.at[d], sz_r.at[o], {"seq": o}).wait_recv()
    acc = sm_z[0]
    for o in range(1, Z):
        acc = acc + sm_z[o]
    smalls_o[...] = acc

    for a in range(5):
        for d in range(1, chips):
            own_copy(a, (chip + d) % chips).wait_send()
    for d in range(1, G):
        o = (m + d) % G
        rcopy(dkv.at[o], mbuf.at[m], mb_s.at[d, 0], mb_r.at[m, 0], {"shard": o * 8 + j}).wait_send()
    exchange_sent(dqt, hq, hq_s, hq_r)
    exchange_sent(fin, hkv, hk_s, hk_r)
    exchange_sent(finm, hm, hm_s, hm_r)
    for far in range(Z - 1, 0, -1):
        for slot in range(8):
            for way in (0, 1):
                t = z + (2 * way - 1) * far

                @pl.when((t >= 0) & (t < Z))
                def _(way=way, t=t, slot=slot):
                    z_copy(way, t, slot, z_view(slot, t)).wait_send()

    for d in range(1, S):
        p = (s + d) % S
        rcopy(psend.at[p], pgot.at[s], p_s.at[d], p_r.at[s], {"shard": p}).wait_send()
        rcopy(msend.at[p], mgot.at[s], pm_s.at[d], pm_r.at[s], {"shard": p}).wait_send()
        rcopy(sm_mine, sm_all.at[s], sm_s.at[d], sm_r.at[s], {"shard": p}).wait_send()
    for d in range(1, Z):
        rcopy(sm_plane, sm_z.at[z], sz_s.at[d], sz_r.at[z], {"seq": (z + d) % Z}).wait_send()
    for k in range(NC):
        r = root(k)
        for step, beyond in ((-1, z > r), (1, z < r)):

            @pl.when(beyond)
            def _(step=step):
                inward(k, step).wait_send()

        for step in (-1, 1):
            sends = (z >= r) & (z < Z - 1) if step > 0 else (z <= r) & (z > 0)

            @pl.when(sends)
            def _(step=step):
                outward(k, step).wait_send()


def finish_kernel(
    info, timestep, zfin, sums, hid_g, enc_g, lay,
    lay_o, hid_o, enc_o, time_o, gain_o, shift_o, proj_o, out_o, cq_o, mem_o, co_o, up_o, upb_o, dn_o, dnb_o,
):
    s = info[3]
    R, F = out_o.shape[0], upb_o.shape[1]
    lay_o[...] = lay[...]
    hid_o[...] = hid_g[...]
    enc_o[...] = enc_g[...]
    out_o[...] = zfin[0].astype(F32)
    cq_o[...] = zfin[1].astype(F32)
    co_o[...] = zfin[2].astype(F32)
    for c in range(4):
        up_o[:, 512 * c : 512 * (c + 1)] = zfin[3 + c].astype(F32)
        dn_o[c * R : (c + 1) * R, :] = zfin[7 + c].astype(F32)
    for c in range(3):
        proj_o[:, 512 * c : 512 * (c + 1)] = zfin[11 + c].astype(F32)
    for c in range(2):
        mem_o[:, 512 * c : 512 * (c + 1)] = zfin[14 + c].astype(F32)

    def own(width, first):
        row = lax.broadcasted_iota(jnp.int32, (512, width), 0)
        col = lax.broadcasted_iota(jnp.int32, (512, width), 1)
        pick = jnp.where(row == col + first, 1.0, 0.0)
        return lax.dot_general(
            sums[...], pick, (((1,), (0,)), ((), ())),
            preferred_element_type=F32, precision=lax.Precision.HIGHEST,
        )

    mine = own(R, s * R)
    gain_o[...] = mine[0:3]
    shift_o[...] = mine[3:6]
    dnb_o[...] = mine[8:9]
    step = lax.broadcasted_iota(jnp.int32, time_o.shape, 0)
    grad = jnp.zeros(time_o.shape, F32)
    for d in range(DOCS):
        grad = grad + jnp.where(step == timestep[d], mine[6 + d : 7 + d], 0.0)
    time_o[...] = grad
    wide = own(F, (s * F) % 512)
    row = lax.broadcasted_iota(jnp.int32, wide.shape, 0)
    upb_o[...] = jnp.sum(jnp.where(row == 9 + s * F // 512, wide, 0.0), axis=0, keepdims=True)


def last(v):
    S, Z, G = v["S"], v["Z"], v["G"]
    T, R, F, E = v["T"], v["R"], v["F"], v["encoder"].shape[0]
    FF = v["wup"].shape[1]
    chips = S // 2
    sds = jax.ShapeDtypeStruct
    V = pltpu.VMEM
    GM, ZM = (G, Z) if G > 1 else (1, 1)
    hidden_grad, encoder_grad, zfin, sums = remote_call(
        functools.partial(last_kernel, S, Z, G),
        "gradients_home",
        4,
        (
            v["info"], v["hidden_in"], v["vecs"], v["d_after"], v["x_all"], v["enc_all"], v["dqt"],
            v["dkv"].reshape(G, 8, Z, T, 128), v["dmem"],
            v["gproj"].reshape(512, 1536), v["gmem"].reshape(512, 1024),
            v["wout_grad"], v["cq_grad"], v["co_grad"], v["up_grad"], v["dn_grad"],
            v["small2"], v["small3"], v["upb_grad"],
        ),
        [sds((T, 512), F32), sds((E, 512), F32), sds((NC, R, 512), BF), sds((16, 512), F32)],
        [V((chips, R, 512), BF)] * 3 + [V((chips, R, FF), BF), V((chips, F, 512), BF)]
        + [
            V((2, Z, 8, T, 128), BF), V((8, T, 128), BF), V((GM, 8, ZM, T, 128), BF),
            V((8, T, 128), BF), V((8, HD, T), BF), V((8, E, 128), BF),
            V((512, 8 * T), BF), V((512, 8 * E), BF), V((8 * T, 256), BF),
            V((S, R, 256), BF), V((S, R, 256), BF), V((S, R, 128), BF), V((S, R, 128), BF),
            V((NC, R, 512), BF), V((2, NC, R, 512), BF),
            V((S, 16, 512), F32), V((Z, 16, 512), F32), V((16, 512), F32), V((16, 512), F32),
            DMA((5, chips)), DMA((5, chips)),
            DMA((2, Z, 8)), DMA((2, Z, 8)), DMA((G, 1)), DMA((G, 1)),
            DMA((8,)), DMA((8,)), DMA((8,)), DMA((8,)), DMA((8,)), DMA((8,)),
            DMA((S,)), DMA((S,)), DMA((S,)), DMA((S,)),
            DMA((2, NC)), DMA((2, NC)), DMA((2, NC)), DMA((NC,)),
            DMA((S,)), DMA((S,)), DMA((Z,)), DMA((Z,)),
        ],
        far=(7,) if G > 1 else (),
    )
    vmem = pl.BlockSpec(memory_space=pltpu.VMEM)
    smem = pl.BlockSpec(memory_space=pltpu.SMEM)
    steps = v["time_table"].shape[0]
    outs = [
        sds((T, 512), BF), sds((T, 512), F32), sds((E, 512), F32), sds((steps, R), F32), sds((3, R), F32),
        sds((3, R), F32), sds((R, 1536), F32), sds((R, 512), F32), sds((R, 512), F32), sds((R, 1024), F32),
        sds((R, 512), F32), sds((R, FF), F32), sds((1, F), F32), sds((F, 512), F32), sds((1, R), F32),
    ]
    res = pl.pallas_call(
        finish_kernel,
        out_shape=outs,
        in_specs=[smem, smem] + [vmem] * 5,
        out_specs=[vmem] * len(outs),
        compiler_params=pltpu.CompilerParams(vmem_limit_bytes=room()),
        name="outputs",
    )(v["info"], v["timestep"], zfin, sums, hidden_grad, encoder_grad, v["layer_out"])
    res = list(res)
    res[12] = res[12].reshape(F)
    res[14] = res[14].reshape(R)
    return tuple(res)


def shards(
    hidden_in, encoder, segment_ids, timestep, out_grad, time_table, norm_gain, norm_bias,
    self_proj, self_out, cross_query, cross_memory, cross_out, up_weight, up_bias, down_weight, down_bias,
):
    S, Z = lax.axis_size("shard"), lax.axis_size("seq")
    T, R, F = hidden_in.shape[0], self_proj.shape[0], up_bias.shape[0]
    G = S // 8
    info, x_all, kv, qt, mem, enc_all, vecs, upb, gout, gcq, gco, gup, gdn = gather_call(
        S,
        Z,
        (
            timestep, segment_ids.reshape(-1, 128), hidden_in, time_table, norm_gain, norm_bias,
            up_bias, down_bias, self_proj, cross_memory, encoder,
            self_out, cross_query, cross_out, up_weight, down_weight,
        ),
    )
    wout, wcq, wco = gout.reshape(512, 512), gcq.reshape(512, 512), gco.reshape(512, 512)
    wup, wdn = gup.reshape(512, -1), gdn.reshape(-1, 512)
    kv = kv.reshape(S * Z, T, 128)

    ot, of, lse = attend(Z, True, info, qt, kv)
    at, after, n2, cqt, mkv = middle(G, Z, info, ot, hidden_in, vecs, wout, wcq, mem)
    mkv = mkv.reshape(DOCS * ENC // T, T, 128)
    crt, crf, clse = attend(Z, False, info, cqt, mkv)
    layer_out, d_after2, co_grad, up_grad, dn_grad, small3, upb_grad, dct, gproj, gmem = feed(
        crt, after, vecs, upb, wco, wup, wdn, out_grad, self_proj, cross_memory
    )
    dcqt, dmkv = attend_back(Z, False, info, cqt, mkv, dct, crf, clse)
    d_after, cq_grad, wout_grad, small2, dat, dmem = middle_back(
        dcqt, after, d_after2, n2, at, vecs, wcq, wout, dmkv.reshape(G, 8, Z, -1, 128)
    )
    dqt, dkv = attend_back(Z, True, info, qt, kv, dat, of, lse)
    return last(locals())


def solution(mesh):
    return jax.shard_map(
        shards,
        mesh=mesh,
        in_specs=(
            P(("shard", "seq"), None),
            P(("shard", "seq"), None),
            P(),
            P(),
            P(("shard", "seq"), None),
            P(None, "shard"),
            P(None, "shard"),
            P(None, "shard"),
            P("shard", None),
            P("shard", None),
            P("shard", None),
            P("shard", None),
            P("shard", None),
            P("shard", None),
            P("shard"),
            P("shard", None),
            P("shard"),
        ),
        out_specs=(
            P(("shard", "seq"), None),
            P(("shard", "seq"), None),
            P(("shard", "seq"), None),
            P(None, "shard"),
            P(None, "shard"),
            P(None, "shard"),
            P("shard", None),
            P("shard", None),
            P("shard", None),
            P("shard", None),
            P("shard", None),
            P("shard", None),
            P("shard"),
            P("shard", None),
            P("shard"),
        ),
        check_vma=False,
    )
```

profile of v0, /device:TPU:0, one launch (start us, length us, event | category | flops | bytes accessed | tf_op | source)
XLA Modules:
  0.0 260.1 jit_solution(10505714022419172193)
XLA Ops:
  0.7 0.0 copy-start
  0.7 0.0 copy-start.4
  0.7 0.7 copy-done.4
  1.4 59.3 %gather_qkv.1 = (s32[4]{0:T(128)S(1)}, bf16[8,256,512]{2,1,0:T(8,128)(2,1)S(1)}, bf16[1,8,4,256,128]{4,3,2,1,0:T(8,128)(2,1)S(1)}, bf16[8,64,256]{2,1,0:T(8,128)...) custom-call(s32[2]{0:T(128)S(1)} %copy-done.4, ...), custom_call_target="tpu_custom_call" | custom-call | tf_op jit(solution)/shard_map/gather_qkv/pallas_call | solution.py:425
  60.6 0.0 copy-start.1
  60.7 0.0 copy-start.2
  60.7 0.0 copy-start.3
  60.7 20.3 %attend_self.1 = (bf16[8,64,256]{2,1,0:T(8,128)(2,1)S(1)}, f32[8,64,256]{2,1,0:T(8,128)S(1)}, f32[8,1,256]{2,1,0:T(1,128)S(1)}) custom-call(s32[4]{0:T(128)S(1)} %get-tuple-element.78.info.bnd, bf16[8,64,256]{2,1,0:T(8,128)(2,1)S(1)} %get-tuple-element.80.qt, bf16[32,256,128]{2,1,0:T(8,128)(2,1)S(1)} %bitcast.14), custom_call_target="tpu_custom_call" | custom-call | tf_op jit(solution)/shard_map/attend_self/pallas_call | solution.py:588
  81.0 0.0 copy-done
  81.0 13.9 %middle.1 = (bf16[8,64,256]{2,1,0:T(8,128)(2,1)S(1)}, f32[256,512]{1,0:T(8,128)S(1)}, bf16[256,512]{1,0:T(8,128)(2,1)S(1)}, bf16[8,64,256]{2,1,0:T(8,128)(2,1)S(1)}, bf16[1,8,4,64,128]{4,3,2,1,0:T(8,128)(2,1)S(1)}) custom-call(s32[4]{0:T(128)S(1)} %get-tuple-element.78.info.bnd, bf16[8,64,256]{2,1,0:T(8,128)(2,1)S(1)} %get-tuple-element.82.ot, ...), custom_call_target="tpu_custom_call" | custom-call | tf_op jit(solution)/shard_map/middle/pallas_call | solution.py:787
  94.9 7.8 %attend_cross.1 = (bf16[8,64,256]{2,1,0:T(8,128)(2,1)S(1)}, f32[8,64,256]{2,1,0:T(8,128)S(1)}, f32[8,1,256]{2,1,0:T(1,128)S(1)}) custom-call(s32[4]{0:T(128)S(1)} %get-tuple-element.78.info.bnd, bf16[8,64,256]{2,1,0:T(8,128)(2,1)S(1)} %get-tuple-element.86.qt, bf16[8,256,128]{2,1,0:T(8,128)(2,1)S(1)} %bitcast.19), custom_call_target="tpu_custom_call" | custom-call | tf_op jit(solution)/shard_map/attend_cross/pallas_call | solution.py:588
  102.7 0.0 copy-done.1
  102.7 0.0 copy-done.2
  102.7 0.0 copy-done.3
  102.7 21.6 %feed_forward.1 = (bf16[256,512]{1,0:T(8,128)(2,1)S(1)}, f32[256,512]{1,0:T(8,128)S(1)}, bf16[4,64,512]{2,1,0:T(8,128)(2,1)S(1)}, bf16[4,64,2048]{2,1,0:T(8,128)...) custom-call(bf16[8,64,256]{2,1,0:T(8,128)(2,1)S(1)} %get-tuple-eleme, ...), custom_call_target="tpu_custom_call" | custom-call | tf_op jit(solution)/shard_map/feed_forward/pallas_call | solution.py:787
  124.3 11.1 %attend_cross_back.1 = (bf16[8,64,256]{2,1,0:T(8,128)(2,1)S(1)}, bf16[8,256,128]{2,1,0:T(8,128)(2,1)S(1)}) custom-call(s32[4]{0:T(128)S(1)} %get-tuple-element.78.info.bnd, bf16[8,64,256]{2,1,0:T(8,128)(2,1)S(1)} %get-tuple-element.86.qt, bf16[8,256,128]{2,1,0:T(8,128)(2,1)S(1)} %bitcast.20, bf16[8,64,256]{2,1,0:T(8,128)(2,1)S(1)} %get-tuple-element.94.dt, ...), custom_call_target="tpu_custom_call" | custom-call | tf_op jit(solution)/shard_map/attend_cross_back/pallas_call | solution.py:676
  135.3 13.8 %middle_back.1 = (f32[256,512]{1,0:T(8,128)S(1)}, bf16[4,64,512]{2,1,0:T(8,128)(2,1)S(1)}, bf16[4,64,512]{2,1,0:T(8,128)(2,1)S(1)}, f32[8,512]{1,0:T(8,128)S(1)}...) custom-call(bf16[8,64,256]{2,1,0:T(8,128)(2,1)S(1)} %get-tuple-element.97.dcqt, ...), custom_call_target="tpu_custom_call" | custom-call | tf_op jit(solution)/shard_map/middle_back/pallas_call | solution.py:787
  149.1 28.9 %attend_self_back.1 = (bf16[8,64,256]{2,1,0:T(8,128)(2,1)S(1)}, bf16[32,256,128]{2,1,0:T(8,128)(2,1)S(1)}) custom-call(s32[4]{0:T(128)S(1)} %get-tuple-element.78.info.bnd, bf16[8,64,256]{2,1,0:T(8,128)(2,1)S(1)} %get-tuple-element.80.qt, bf16[32,256,128]{2,1,0:T(8,128)(2,1)S(1)} %bitcast.15, bf16[8,64,256]{2,1,0:T(8,128)(2,1)S(1)} %get-tuple-element.105.dt, ...), custom_call_target="tpu_custom_call" | custom-call | tf_op jit(solution)/shard_map/attend_self_back/pallas_call | solution.py:676
  178.0 0.0 copy-start.5
  178.0 79.4 %gradients_home.1 = (f32[256,512]{1,0:T(8,128)S(1)}, f32[64,512]{1,0:T(8,128)S(1)}, bf16[16,64,512]{2,1,0:T(8,128)(2,1)S(1)}, f32[16,512]{1,0:T(8,128)S(1)}) custom-call(s32[4]{0:T(128)S(1)} %get-tuple-element.78.info.bnd, bf16[256,512]{1,0:T(8,128)(2,1)S(1)} %copy-done, f32[16,512]{1,0:T(8,128)S(1)} %get-tuple-element.79.vecs, ...), custom_call_target="tpu_custom_call" | custom-call | tf_op jit(solution)/shard_map/gradients_home/pallas_call | solution.py:787
  257.4 0.0 copy-done.5
  257.4 2.6 %outputs.1 = (bf16[256,512]{1,0:T(8,128)(2,1)}, f32[256,512]{1,0:T(8,128)}, f32[64,512]{1,0:T(8,128)}, f32[50,64]{1,0:T(8,128)}, f32[3,64]{1,0:T(4,128)}, /*inde...) custom-call(s32[4]{0:T(128)S(1)} %get-tuple-element.78.info.bnd, ...), custom_call_target="tpu_custom_call" | custom-call | tf_op jit(solution)/shard_map/outputs/pallas_call | solution.py:1502
Async XLA Ops:
  0.7 80.3 %copy-start = (bf16[256,512]{1,0:T(8,128)(2,1)S(1)}, bf16[256,512]{1,0:T(8,128)(2,1)}, u32[]{:S(2)}) copy-start(bf16[256,512]{1,0:T(8,128)(2,1)} %hid.3) | copy-start | bytes 786436
  0.7 0.7 copy-start.4
  60.6 42.0 %copy-start.1 = (bf16[64,1536]{1,0:T(8,128)(2,1)S(1)}, bf16[64,1536]{1,0:T(8,128)(2,1)}, u32[]{:S(2)}) copy-start(bf16[64,1536]{1,0:T(8,128)(2,1)} %wproj.1) | copy-start | bytes 589828
  60.7 42.0 %copy-start.2 = (bf16[64,1024]{1,0:T(8,128)(2,1)S(1)}, bf16[64,1024]{1,0:T(8,128)(2,1)}, u32[]{:S(2)}) copy-start(bf16[64,1024]{1,0:T(8,128)(2,1)} %wmem.1) | copy-start | bytes 393220
  60.7 42.0 %copy-start.3 = (bf16[256,512]{1,0:T(8,128)(2,1)S(1)}, bf16[256,512]{1,0:T(8,128)(2,1)}, u32[]{:S(2)}) copy-start(bf16[256,512]{1,0:T(8,128)(2,1)} %grad.1) | copy-start | bytes 786436
  178.0 79.4 %copy-start.5 = (s32[2]{0:T(128)S(1)}, s32[2]{0:T(128)}, u32[]{:S(2)}) copy-start(s32[2]{0:T(128)} %timestep.3) | copy-start | bytes 28
where the time goes:
time: 263 us; the launch traced here: 260 us
  Pallas kernels  258 us (98%)
    pallas_call x4, Pallas kernels, remote_call(): pl.pallas_call(kernel, out_shape=outs, in_specs=in_specs, out_specs=out_s...  129 us
    pallas_call x1, Pallas kernels, gather_call(): pl.pallas_call(functools.partial(gather_kernel, S, Z, G), out_shape=outs,...  59.3 us
    pallas_call x2, Pallas kernels, attend_back(): pl.pallas_call(functools.partial(attend_back_kernel, Z, causal), out_shap...  39.9 us
    pallas_call x2, Pallas kernels, attend(): pl.pallas_call(functools.partial(attend_kernel, Z, causal), out_shape=[sd...  28.1 us

commit v1 on v0

--- a/solution.py
+++ b/solution.py
@@ -365,7 +365,7 @@
         for b in range(8):
             mkv[b] = mm(enc_all[b], m_head).astype(BF)
 
-    lag = 2
+    lag = 3
     last_step = max(8, 7 + lag * (Z - 1))
     for n in range(last_step + 1):
         if n < 8:
@@ -627,17 +627,17 @@
         level = lse[i]
 
         def group(kind, start, limit, acc):
-            keys = kv[pl.ds(start, GROUP)].reshape(GROUP * T, 128)
-            raw[...] = mm(keys, qd[...])
+            for n in range(GROUP):
+                raw[n * T : (n + 1) * T] = mm(kv[start + n], qd[...])
             for n in range(GROUP):
                 at = slice(n * T, (n + 1) * T)
                 probs = jnp.exp(reach.mask(kind, start, limit, n, raw[at, :T]) - level)
                 pair[at, :T] = probs.astype(BF)
                 pair[at, T:] = (probs * (raw[at, T:] - delta)).astype(BF)
-            grads = mm(pair[...], rows[...])
-            dkvf[pl.ds(start, GROUP)] += grads.reshape(GROUP, T, 128)
-            flat = kt[:, pl.ds(pl.multiple_of(start * T, T), GROUP * T)]
-            return acc + mm(flat, pair[:, T:])
+                dkvf[start + n] += mm(pair[at], rows[...])
+                flat = kt[:, pl.ds(pl.multiple_of((start + n) * T, T), T)]
+                acc = acc + mm(flat, pair[at, T:])
+            return acc
 
         acc = reach.walk(group, jnp.zeros((HD, T), F32))
         dq[i] = (SCALE * acc).astype(BF)
@@ -1341,6 +1341,8 @@
         total_of(k)
     for k in range(6):
         send_out(k)
+    for k in range(11, NC):
+        partial(k)
     e_keys = jnp.concatenate([hm[h][:, :HD] for h in range(H)], axis=1)
     e_values = jnp.concatenate([hm[h][:, HD:] for h in range(H)], axis=1)
     encoder_grad[...] = mm(e_keys, wmem[:, :512], 1, 1) + mm(e_values, wmem[:, 512:], 1, 1)
@@ -1356,10 +1358,8 @@
         rcopy(sm_plane, sm_z.at[z], sz_s.at[d], sz_r.at[z], {"seq": (z + d) % Z}).start()
     sm_z[z] = acc
     for k in range(11, NC):
-        partial(k)
+        total_of(k)
         send_out(k - 5)
-    for k in range(11, NC):
-        total_of(k)
     for k in range(11, NC):
         send_out(k)
     for d in range(1, Z):

time: 263 us -> 259 us (0.985)
  no operation moved by 1% of the time
where the time goes in v1:
time: 259 us
  Pallas kernels  257 us (99%)
    pallas_call x4, Pallas kernels, remote_call(): pl.pallas_call(kernel, out_shape=outs, in_specs=in_specs, out_specs=out_s...  129 us
    pallas_call x1, Pallas kernels, gather_call(): pl.pallas_call(functools.partial(gather_kernel, S, Z, G), out_shape=outs,...  58.5 us
    pallas_call x2, Pallas kernels, attend_back(): pl.pallas_call(functools.partial(attend_back_kernel, Z, causal), out_shap...  38.6 us
    pallas_call x2, Pallas kernels, attend(): pl.pallas_call(functools.partial(attend_kernel, Z, causal), out_shape=[sd...  28 us

profile of v1, /device:TPU:0, one launch (start us, length us, event | category | flops | bytes accessed | tf_op | source)
XLA Modules:
  0.0 258.5 jit_solution(5548151245534866313)
XLA Ops:
  0.7 0.0 copy-start
  0.7 0.0 copy-start.4
  0.7 0.7 copy-done.4
  1.4 58.5 %gather_qkv.1 = (s32[4]{0:T(128)S(1)}, bf16[8,256,512]{2,1,0:T(8,128)(2,1)S(1)}, bf16[1,8,4,256,128]{4,3,2,1,0:T(8,128)(2,1)S(1)}, bf16[8,64,256]{2,1,0:T(8,128)...) custom-call(s32[2]{0:T(128)S(1)} %copy-done.4, ...), custom_call_target="tpu_custom_call" | custom-call | tf_op jit(solution)/shard_map/gather_qkv/pallas_call | solution.py:425
  59.9 0.0 copy-start.1
  59.9 0.0 copy-start.2
  59.9 0.0 copy-start.3
  59.9 20.2 %attend_self.1 = (bf16[8,64,256]{2,1,0:T(8,128)(2,1)S(1)}, f32[8,64,256]{2,1,0:T(8,128)S(1)}, f32[8,1,256]{2,1,0:T(1,128)S(1)}) custom-call(s32[4]{0:T(128)S(1)} %get-tuple-element.78.info.bnd, bf16[8,64,256]{2,1,0:T(8,128)(2,1)S(1)} %get-tuple-element.80.qt, bf16[32,256,128]{2,1,0:T(8,128)(2,1)S(1)} %bitcast.14), custom_call_target="tpu_custom_call" | custom-call | tf_op jit(solution)/shard_map/attend_self/pallas_call | solution.py:588
  80.1 0.0 copy-done
  80.1 13.9 %middle.1 = (bf16[8,64,256]{2,1,0:T(8,128)(2,1)S(1)}, f32[256,512]{1,0:T(8,128)S(1)}, bf16[256,512]{1,0:T(8,128)(2,1)S(1)}, bf16[8,64,256]{2,1,0:T(8,128)(2,1)S(1)}, bf16[1,8,4,64,128]{4,3,2,1,0:T(8,128)(2,1)S(1)}) custom-call(s32[4]{0:T(128)S(1)} %get-tuple-element.78.info.bnd, bf16[8,64,256]{2,1,0:T(8,128)(2,1)S(1)} %get-tuple-element.82.ot, ...), custom_call_target="tpu_custom_call" | custom-call | tf_op jit(solution)/shard_map/middle/pallas_call | solution.py:787
  94.1 7.8 %attend_cross.1 = (bf16[8,64,256]{2,1,0:T(8,128)(2,1)S(1)}, f32[8,64,256]{2,1,0:T(8,128)S(1)}, f32[8,1,256]{2,1,0:T(1,128)S(1)}) custom-call(s32[4]{0:T(128)S(1)} %get-tuple-element.78.info.bnd, bf16[8,64,256]{2,1,0:T(8,128)(2,1)S(1)} %get-tuple-element.86.qt, bf16[8,256,128]{2,1,0:T(8,128)(2,1)S(1)} %bitcast.19), custom_call_target="tpu_custom_call" | custom-call | tf_op jit(solution)/shard_map/attend_cross/pallas_call | solution.py:588
  101.9 0.0 copy-done.1
  101.9 0.0 copy-done.2
  101.9 0.0 copy-done.3
  101.9 21.4 %feed_forward.1 = (bf16[256,512]{1,0:T(8,128)(2,1)S(1)}, f32[256,512]{1,0:T(8,128)S(1)}, bf16[4,64,512]{2,1,0:T(8,128)(2,1)S(1)}, bf16[4,64,2048]{2,1,0:T(8,128)...) custom-call(bf16[8,64,256]{2,1,0:T(8,128)(2,1)S(1)} %get-tuple-eleme, ...), custom_call_target="tpu_custom_call" | custom-call | tf_op jit(solution)/shard_map/feed_forward/pallas_call | solution.py:787
  123.3 10.7 %attend_cross_back.1 = (bf16[8,64,256]{2,1,0:T(8,128)(2,1)S(1)}, bf16[8,256,128]{2,1,0:T(8,128)(2,1)S(1)}) custom-call(s32[4]{0:T(128)S(1)} %get-tuple-element.78.info.bnd, bf16[8,64,256]{2,1,0:T(8,128)(2,1)S(1)} %get-tuple-element.86.qt, bf16[8,256,128]{2,1,0:T(8,128)(2,1)S(1)} %bitcast.20, bf16[8,64,256]{2,1,0:T(8,128)(2,1)S(1)} %get-tuple-element.94.dt, ...), custom_call_target="tpu_custom_call" | custom-call | tf_op jit(solution)/shard_map/attend_cross_back/pallas_call | solution.py:676
  134.0 13.8 %middle_back.1 = (f32[256,512]{1,0:T(8,128)S(1)}, bf16[4,64,512]{2,1,0:T(8,128)(2,1)S(1)}, bf16[4,64,512]{2,1,0:T(8,128)(2,1)S(1)}, f32[8,512]{1,0:T(8,128)S(1)}...) custom-call(bf16[8,64,256]{2,1,0:T(8,128)(2,1)S(1)} %get-tuple-element.97.dcqt, ...), custom_call_target="tpu_custom_call" | custom-call | tf_op jit(solution)/shard_map/middle_back/pallas_call | solution.py:787
  147.8 27.9 %attend_self_back.1 = (bf16[8,64,256]{2,1,0:T(8,128)(2,1)S(1)}, bf16[32,256,128]{2,1,0:T(8,128)(2,1)S(1)}) custom-call(s32[4]{0:T(128)S(1)} %get-tuple-element.78.info.bnd, bf16[8,64,256]{2,1,0:T(8,128)(2,1)S(1)} %get-tuple-element.80.qt, bf16[32,256,128]{2,1,0:T(8,128)(2,1)S(1)} %bitcast.15, bf16[8,64,256]{2,1,0:T(8,128)(2,1)S(1)} %get-tuple-element.105.dt, ...), custom_call_target="tpu_custom_call" | custom-call | tf_op jit(solution)/shard_map/attend_self_back/pallas_call | solution.py:676
  175.7 0.0 copy-start.5
  175.7 80.0 %gradients_home.1 = (f32[256,512]{1,0:T(8,128)S(1)}, f32[64,512]{1,0:T(8,128)S(1)}, bf16[16,64,512]{2,1,0:T(8,128)(2,1)S(1)}, f32[16,512]{1,0:T(8,128)S(1)}) custom-call(s32[4]{0:T(128)S(1)} %get-tuple-element.78.info.bnd, bf16[256,512]{1,0:T(8,128)(2,1)S(1)} %copy-done, f32[16,512]{1,0:T(8,128)S(1)} %get-tuple-element.79.vecs, ...), custom_call_target="tpu_custom_call" | custom-call | tf_op jit(solution)/shard_map/gradients_home/pallas_call | solution.py:787
  255.7 0.0 copy-done.5
  255.8 2.6 %outputs.1 = (bf16[256,512]{1,0:T(8,128)(2,1)}, f32[256,512]{1,0:T(8,128)}, f32[64,512]{1,0:T(8,128)}, f32[50,64]{1,0:T(8,128)}, f32[3,64]{1,0:T(4,128)}, /*inde...) custom-call(s32[4]{0:T(128)S(1)} %get-tuple-element.78.info.bnd, ...), custom_call_target="tpu_custom_call" | custom-call | tf_op jit(solution)/shard_map/outputs/pallas_call | solution.py:1502
Async XLA Ops:
  0.7 79.5 %copy-start = (bf16[256,512]{1,0:T(8,128)(2,1)S(1)}, bf16[256,512]{1,0:T(8,128)(2,1)}, u32[]{:S(2)}) copy-start(bf16[256,512]{1,0:T(8,128)(2,1)} %hid.3) | copy-start | bytes 786436
  0.7 0.7 copy-start.4
  59.9 42.0 %copy-start.1 = (bf16[64,1536]{1,0:T(8,128)(2,1)S(1)}, bf16[64,1536]{1,0:T(8,128)(2,1)}, u32[]{:S(2)}) copy-start(bf16[64,1536]{1,0:T(8,128)(2,1)} %wproj.1) | copy-start | bytes 589828
  59.9 42.0 %copy-start.2 = (bf16[64,1024]{1,0:T(8,128)(2,1)S(1)}, bf16[64,1024]{1,0:T(8,128)(2,1)}, u32[]{:S(2)}) copy-start(bf16[64,1024]{1,0:T(8,128)(2,1)} %wmem.1) | copy-start | bytes 393220
  59.9 42.0 %copy-start.3 = (bf16[256,512]{1,0:T(8,128)(2,1)S(1)}, bf16[256,512]{1,0:T(8,128)(2,1)}, u32[]{:S(2)}) copy-start(bf16[256,512]{1,0:T(8,128)(2,1)} %grad.1) | copy-start | bytes 786436
  175.7 80.0 %copy-start.5 = (s32[2]{0:T(128)S(1)}, s32[2]{0:T(128)}, u32[]{:S(2)}) copy-start(s32[2]{0:T(128)} %timestep.3) | copy-start | bytes 28

commit v2 on v1

--- a/solution.py
+++ b/solution.py
@@ -372,7 +372,7 @@
             block_step(n)
         if n == 8:
             encoder_step()
-        if n == 5:
+        if n == 3:
             for a in range(5):
                 whole.start(a)
         for hop in range(1, Z):

time: 259 us -> 260 us (level)
    pallas_call x4, Pallas kernels: 129 us -> 136 us  [remote_call(): pl.pallas_call(kernel, out_shape=outs, in_specs=in_specs, out_specs=out_s...]
    pallas_call x2, Pallas kernels: 38.6 us -> 34.5 us  [attend_back(): pl.pallas_call(functools.partial(attend_back_kernel, Z, causal), out_shap...]
    pallas_call x2, Pallas kernels: 28 us -> 24.6 us  [attend(): pl.pallas_call(functools.partial(attend_kernel, Z, causal), out_shape=[sd...]
where the time goes in v2:
time: 260 us; the launch traced here: 258 us
  Pallas kernels  256 us (98%)
    pallas_call x4, Pallas kernels, remote_call(): pl.pallas_call(kernel, out_shape=outs, in_specs=in_specs, out_specs=out_s...  136 us
    pallas_call x1, Pallas kernels, gather_call(): pl.pallas_call(functools.partial(gather_kernel, S, Z, G), out_shape=outs,...  58.5 us
    pallas_call x2, Pallas kernels, attend_back(): pl.pallas_call(functools.partial(attend_back_kernel, Z, causal), out_shap...  34.5 us
    pallas_call x2, Pallas kernels, attend(): pl.pallas_call(functools.partial(attend_kernel, Z, causal), out_shape=[sd...  24.6 us

profile of v2, /device:TPU:0, one launch (start us, length us, event | category | flops | bytes accessed | tf_op | source)
XLA Modules:
  0.0 257.6 jit_solution(4910079579510385326)
XLA Ops:
  0.7 0.0 copy-start
  0.7 0.0 copy-start.4
  0.7 0.7 copy-done.4
  1.4 58.5 %gather_qkv.1 = (s32[4]{0:T(128)S(1)}, bf16[8,256,512]{2,1,0:T(8,128)(2,1)S(1)}, bf16[1,8,4,256,128]{4,3,2,1,0:T(8,128)(2,1)S(1)}, bf16[8,64,256]{2,1,0:T(8,128)...) custom-call(s32[2]{0:T(128)S(1)} %copy-done.4, ...), custom_call_target="tpu_custom_call" | custom-call | tf_op jit(solution)/shard_map/gather_qkv/pallas_call | solution.py:425
  59.9 0.0 copy-start.1
  59.9 0.0 copy-start.2
  59.9 0.0 copy-start.3
  59.9 17.9 %attend_self.1 = (bf16[8,64,256]{2,1,0:T(8,128)(2,1)S(1)}, f32[8,64,256]{2,1,0:T(8,128)S(1)}, f32[8,1,256]{2,1,0:T(1,128)S(1)}) custom-call(s32[4]{0:T(128)S(1)} %get-tuple-element.78.info.bnd, bf16[8,64,256]{2,1,0:T(8,128)(2,1)S(1)} %get-tuple-element.80.qt, bf16[32,256,128]{2,1,0:T(8,128)(2,1)S(1)} %bitcast.14), custom_call_target="tpu_custom_call" | custom-call | tf_op jit(solution)/shard_map/attend_self/pallas_call | solution.py:588
  77.8 0.0 copy-done
  77.9 13.9 %middle.1 = (bf16[8,64,256]{2,1,0:T(8,128)(2,1)S(1)}, f32[256,512]{1,0:T(8,128)S(1)}, bf16[256,512]{1,0:T(8,128)(2,1)S(1)}, bf16[8,64,256]{2,1,0:T(8,128)(2,1)S(1)}, bf16[1,8,4,64,128]{4,3,2,1,0:T(8,128)(2,1)S(1)}) custom-call(s32[4]{0:T(128)S(1)} %get-tuple-element.78.info.bnd, bf16[8,64,256]{2,1,0:T(8,128)(2,1)S(1)} %get-tuple-element.82.ot, ...), custom_call_target="tpu_custom_call" | custom-call | tf_op jit(solution)/shard_map/middle/pallas_call | solution.py:787
  91.8 6.7 %attend_cross.1 = (bf16[8,64,256]{2,1,0:T(8,128)(2,1)S(1)}, f32[8,64,256]{2,1,0:T(8,128)S(1)}, f32[8,1,256]{2,1,0:T(1,128)S(1)}) custom-call(s32[4]{0:T(128)S(1)} %get-tuple-element.78.info.bnd, bf16[8,64,256]{2,1,0:T(8,128)(2,1)S(1)} %get-tuple-element.86.qt, bf16[8,256,128]{2,1,0:T(8,128)(2,1)S(1)} %bitcast.19), custom_call_target="tpu_custom_call" | custom-call | tf_op jit(solution)/shard_map/attend_cross/pallas_call | solution.py:588
  98.5 0.0 copy-done.1
  98.5 0.0 copy-done.2
  98.5 0.0 copy-done.3
  98.5 21.4 %feed_forward.1 = (bf16[256,512]{1,0:T(8,128)(2,1)S(1)}, f32[256,512]{1,0:T(8,128)S(1)}, bf16[4,64,512]{2,1,0:T(8,128)(2,1)S(1)}, bf16[4,64,2048]{2,1,0:T(8,128)...) custom-call(bf16[8,64,256]{2,1,0:T(8,128)(2,1)S(1)} %get-tuple-eleme, ...), custom_call_target="tpu_custom_call" | custom-call | tf_op jit(solution)/shard_map/feed_forward/pallas_call | solution.py:787
  120.0 9.4 %attend_cross_back.1 = (bf16[8,64,256]{2,1,0:T(8,128)(2,1)S(1)}, bf16[8,256,128]{2,1,0:T(8,128)(2,1)S(1)}) custom-call(s32[4]{0:T(128)S(1)} %get-tuple-element.78.info.bnd, bf16[8,64,256]{2,1,0:T(8,128)(2,1)S(1)} %get-tuple-element.86.qt, bf16[8,256,128]{2,1,0:T(8,128)(2,1)S(1)} %bitcast.20, bf16[8,64,256]{2,1,0:T(8,128)(2,1)S(1)} %get-tuple-element.94.dt, ...), custom_call_target="tpu_custom_call" | custom-call | tf_op jit(solution)/shard_map/attend_cross_back/pallas_call | solution.py:676
  129.4 17.3 %middle_back.1 = (f32[256,512]{1,0:T(8,128)S(1)}, bf16[4,64,512]{2,1,0:T(8,128)(2,1)S(1)}, bf16[4,64,512]{2,1,0:T(8,128)(2,1)S(1)}, f32[8,512]{1,0:T(8,128)S(1)}...) custom-call(bf16[8,64,256]{2,1,0:T(8,128)(2,1)S(1)} %get-tuple-element.97.dcqt, ...), custom_call_target="tpu_custom_call" | custom-call | tf_op jit(solution)/shard_map/middle_back/pallas_call | solution.py:787
  146.7 25.1 %attend_self_back.1 = (bf16[8,64,256]{2,1,0:T(8,128)(2,1)S(1)}, bf16[32,256,128]{2,1,0:T(8,128)(2,1)S(1)}) custom-call(s32[4]{0:T(128)S(1)} %get-tuple-element.78.info.bnd, bf16[8,64,256]{2,1,0:T(8,128)(2,1)S(1)} %get-tuple-element.80.qt, bf16[32,256,128]{2,1,0:T(8,128)(2,1)S(1)} %bitcast.15, bf16[8,64,256]{2,1,0:T(8,128)(2,1)S(1)} %get-tuple-element.105.dt, ...), custom_call_target="tpu_custom_call" | custom-call | tf_op jit(solution)/shard_map/attend_self_back/pallas_call | solution.py:676
  171.8 0.0 copy-start.5
  171.8 83.1 %gradients_home.1 = (f32[256,512]{1,0:T(8,128)S(1)}, f32[64,512]{1,0:T(8,128)S(1)}, bf16[16,64,512]{2,1,0:T(8,128)(2,1)S(1)}, f32[16,512]{1,0:T(8,128)S(1)}) custom-call(s32[4]{0:T(128)S(1)} %get-tuple-element.78.info.bnd, bf16[256,512]{1,0:T(8,128)(2,1)S(1)} %copy-done, f32[16,512]{1,0:T(8,128)S(1)} %get-tuple-element.79.vecs, ...), custom_call_target="tpu_custom_call" | custom-call | tf_op jit(solution)/shard_map/gradients_home/pallas_call | solution.py:787
  254.9 0.0 copy-done.5
  254.9 2.6 %outputs.1 = (bf16[256,512]{1,0:T(8,128)(2,1)}, f32[256,512]{1,0:T(8,128)}, f32[64,512]{1,0:T(8,128)}, f32[50,64]{1,0:T(8,128)}, f32[3,64]{1,0:T(4,128)}, /*inde...) custom-call(s32[4]{0:T(128)S(1)} %get-tuple-element.78.info.bnd, ...), custom_call_target="tpu_custom_call" | custom-call | tf_op jit(solution)/shard_map/outputs/pallas_call | solution.py:1502
Async XLA Ops:
  0.7 77.2 %copy-start = (bf16[256,512]{1,0:T(8,128)(2,1)S(1)}, bf16[256,512]{1,0:T(8,128)(2,1)}, u32[]{:S(2)}) copy-start(bf16[256,512]{1,0:T(8,128)(2,1)} %hid.3) | copy-start | bytes 786436
  0.7 0.7 copy-start.4
  59.9 38.6 %copy-start.1 = (bf16[64,1536]{1,0:T(8,128)(2,1)S(1)}, bf16[64,1536]{1,0:T(8,128)(2,1)}, u32[]{:S(2)}) copy-start(bf16[64,1536]{1,0:T(8,128)(2,1)} %wproj.1) | copy-start | bytes 589828
  59.9 38.6 %copy-start.2 = (bf16[64,1024]{1,0:T(8,128)(2,1)S(1)}, bf16[64,1024]{1,0:T(8,128)(2,1)}, u32[]{:S(2)}) copy-start(bf16[64,1024]{1,0:T(8,128)(2,1)} %wmem.1) | copy-start | bytes 393220
  59.9 38.6 %copy-start.3 = (bf16[256,512]{1,0:T(8,128)(2,1)S(1)}, bf16[256,512]{1,0:T(8,128)(2,1)}, u32[]{:S(2)}) copy-start(bf16[256,512]{1,0:T(8,128)(2,1)} %grad.1) | copy-start | bytes 786436
  171.8 83.1 %copy-start.5 = (s32[2]{0:T(128)S(1)}, s32[2]{0:T(128)}, u32[]{:S(2)}) copy-start(s32[2]{0:T(128)} %timestep.3) | copy-start | bytes 28
